TPU v7x, 32 devices: a whole 2x2x4 slice. The times are simulated.
32 devices in a mesh: seq: 2 (over x), fsdp: 16 (over z, y, core).
Axes of the slice: x: 2, y: 2, z: 4, core: 2. Of those that a mesh axis runs over, the one named last changes fastest.
Arguments:
- hidden_in: bfloat16 [2, 2048, 768], P(None, ('seq', 'fsdp')), may hold values from -6 to 6
- time_index: int32 [2], replicated, may hold values from 0 to 999, as said below
- cotangent: bfloat16 [2, 2048, 768], P(None, ('seq', 'fsdp')), may hold values from -6 to 6
- w_qkv: bfloat16 [768, 2304], P('fsdp'), may hold values from -0.21875 to 0.21875
- w_attn_out: bfloat16 [768, 768], P('fsdp'), may hold values from -2 to 2
- w_mlp_in: bfloat16 [768, 3072], P('fsdp'), may hold values from -0.21875 to 0.21875
- w_mlp_out: bfloat16 [3072, 768], P('fsdp'), may hold values from -0.109375 to 0.109375
- w_ada: bfloat16 [4608, 128], P('fsdp'), may hold values from -0.5 to 0.5
- bias_ada: bfloat16 [4608], P('fsdp'), may hold values from -3 to 3
- gain_attn: bfloat16 [768], P('fsdp'), may hold values from 0.5 to 1.5
- gain_mlp: bfloat16 [768], P('fsdp'), may hold values from 0.5 to 1.5
- bias_mlp_in: bfloat16 [3072], P('fsdp'), may hold values from -3 to 3
- bias_mlp_out: bfloat16 [768], P('fsdp'), may hold values from -3 to 3
Outputs:
- output: bfloat16 [2, 2048, 768], P(None, ('seq', 'fsdp'))
- grad_hidden_in: float32 [2, 2048, 768], P(None, ('seq', 'fsdp'))
- grad_w_qkv: float32 [768, 2304], P('fsdp')
- grad_w_attn_out: float32 [768, 768], P('fsdp')
- grad_w_mlp_in: float32 [768, 3072], P('fsdp')
- gradient_mlp_output_weight: float32 [3072, 768], P('fsdp')
- grad_w_ada: float32 [4608, 128], P('fsdp')
- grad_bias_ada: float32 [4608], P('fsdp')
- grad_gain_attn: float32 [768], P('fsdp')
- grad_gain_mlp: float32 [768], P('fsdp')
- grad_bias_mlp_in: float32 [3072], P('fsdp')
- grad_bias_mlp_out: float32 [768], P('fsdp')
Inputs may be any that keep to these rules, and one draw needn't show every extreme that they name: `time_index`: the 2 sequences have different time indices.
All inputs are finite; a program needn't handle non-finite values.
Results may differ from a plain program's by a relative error of at most 0.015.
The roundings to bfloat16 on the way count: a program that leaves them out, or rounds other values in their place, can miss the bound.
Values may be sent and summed in bfloat16 or wider, within the bound.
No kernel may reach another device: no remote copies, remote signals or barrier semaphores. Data moves between devices by JAX's collectives and lax.ppermute only.
A program may use at most 576 MiB of HBM per device.

v0:
```python
import math

import jax
import jax.numpy as jnp
from jax import lax
from jax.experimental import pallas as pl
from jax.experimental.pallas import tpu as pltpu
from jax.sharding import PartitionSpec as P

HEADS = 12
HDIM = 64


highest_precision = lax.Precision.HIGHEST


def normalize(values):
    center = values - jnp.mean(values, -1, keepdims=True)
    return center * lax.rsqrt(jnp.mean(center * center, -1, keepdims=True) + 1e-05)


def adapt(values, gain, shift, scale):
    return normalize(values) * gain * (1.0 + scale) + shift


def time_features(time_index, width):
    half_width = width // 2
    frequency = jnp.exp(-math.log(10000.0) * jnp.arange(half_width, dtype=jnp.float32) / half_width)
    angles = time_index.astype(jnp.float32)[:, None] * frequency[None, :]
    return jnp.concatenate([jnp.cos(angles), jnp.sin(angles)], -1)


def rotary_tables(positions, head_dim):
    inverse = jnp.exp(-math.log(10000.0) * jnp.arange(0, head_dim, 2, dtype=jnp.float32) / head_dim)
    angles = positions.astype(jnp.float32)[:, None] * inverse[None, :]
    angles = jnp.concatenate([angles, angles], -1)
    return (jnp.cos(angles), jnp.sin(angles))


def rotate(values, cosine, sine):
    first_half, second_half = jnp.split(values, 2, axis=-1)
    turned = jnp.concatenate([-second_half, first_half], -1)
    return values * cosine[:, None, :] + turned * sine[:, None, :]


def contract_rows(left_neighbor, right_neighbor):
    return lax.dot_general(
        left_neighbor, right_neighbor, (((0,), (0,)), ((), ())), preferred_element_type=jnp.float32
    )


def contract_cols(left_neighbor, right_neighbor):
    return lax.dot_general(
        left_neighbor, right_neighbor, (((1,), (1,)), ((), ())), preferred_element_type=jnp.float32
    )


def gelu_tanh(values):
    return jax.nn.gelu(values, approximate=True)


def local(
    hidden_in,
    time_index,
    cotangent,
    w_qkv,
    w_attn_out,
    w_mlp_in,
    w_mlp_out,
    w_ada,
    bias_ada,
    gain_attn,
    gain_mlp,
    bias_mlp_in,
    bias_mlp_out,
):
    seqs_here, row_count, width = hidden_in.shape
    flat_rows = seqs_here * row_count
    gathered = (
        lax.all_gather(w_qkv, "fsdp", axis=0, tiled=True),
        lax.all_gather(w_attn_out, "fsdp", axis=0, tiled=True),
        lax.all_gather(w_mlp_in, "fsdp", axis=0, tiled=True),
        lax.all_gather(w_mlp_out, "fsdp", axis=0, tiled=True),
        lax.all_gather(w_ada, "fsdp", axis=0, tiled=True),
        lax.all_gather(bias_ada, "fsdp", axis=0, tiled=True),
        lax.all_gather(gain_attn, "fsdp", axis=0, tiled=True),
        lax.all_gather(gain_mlp, "fsdp", axis=0, tiled=True),
        lax.all_gather(bias_mlp_in, "fsdp", axis=0, tiled=True),
        lax.all_gather(bias_mlp_out, "fsdp", axis=0, tiled=True),
    )
    (
        full_qkv,
        gathered_output,
        full_in,
        full_down,
        full_ada,
        full_bias_ada,
        full_gain_attn,
        full_gain_mlp,
        full_bias_in,
        full_bias_down,
    ) = gathered
    gain_first = full_gain_attn.astype(jnp.float32)
    gain_second = full_gain_mlp.astype(jnp.float32)
    cond = jax.nn.silu(time_features(time_index, full_ada.shape[1]))
    modulation = jnp.dot(
        cond, full_ada.astype(jnp.float32).T, precision=highest_precision
    ) + full_bias_ada.astype(jnp.float32)
    shift_attn, scale_attn, gate_attn, shift_mlp, scale_mlp, gate_mlp = jnp.split(
        modulation[:, None, :], 6, axis=-1
    )
    source = hidden_in.astype(jnp.float32)
    attn_in = adapt(source, gain_first, shift_attn, scale_attn)
    attn_low = attn_in.astype(jnp.bfloat16).reshape(flat_rows, width)
    qkv = jnp.dot(attn_low, full_qkv, preferred_element_type=jnp.float32).reshape(
        seqs_here, row_count, 3 * width
    )
    device_number = lax.axis_index("seq") * lax.axis_size("fsdp") + lax.axis_index("fsdp")
    positions = device_number * row_count + jnp.arange(row_count, dtype=jnp.int32)
    cosine, sine = rotary_tables(positions, HDIM)

    def turn_all(packed):
        split_three = packed.reshape(seqs_here, row_count, 3, HEADS, HDIM)
        query_turned = rotate(split_three[:, :, 0], cosine, sine).reshape(
            seqs_here, row_count, width
        )
        key_turned = rotate(split_three[:, :, 1], cosine, sine).reshape(seqs_here, row_count, width)
        return (query_turned, key_turned, split_three[:, :, 2].reshape(seqs_here, row_count, width))

    query_rot, key_rot, value_raw = turn_all(qkv)
    queries, keys, values = (
        lax.all_to_all(
            query_rot.astype(jnp.bfloat16), "seq", split_axis=2, concat_axis=1, tiled=True
        ),
        lax.all_to_all(
            key_rot.astype(jnp.bfloat16), "seq", split_axis=2, concat_axis=1, tiled=True
        ),
        lax.all_to_all(
            value_raw.astype(jnp.bfloat16), "seq", split_axis=2, concat_axis=1, tiled=True
        ),
    )
    local_heads = HEADS // lax.axis_size("seq")
    span = queries.shape[1]
    query_heads = queries.reshape(seqs_here, span, local_heads, HDIM)
    scale = HDIM ** (-0.5)

    def score_block(key_piece):
        key_heads = key_piece.reshape(seqs_here, key_piece.shape[1], local_heads, HDIM)
        logits = (
            jnp.einsum(
                "sqhd,skhd->shqk", query_heads, key_heads, preferred_element_type=jnp.float32
            )
            * scale
        )
        return (logits, key_heads)

    pieces = (
        lax.all_gather(keys, "fsdp", axis=1, tiled=True),
        lax.all_gather(values, "fsdp", axis=1, tiled=True),
    )
    best = jnp.full((seqs_here, local_heads, span), -1e30, jnp.float32)
    logits, unused = score_block(pieces[0])
    value_heads = pieces[1].reshape(seqs_here, pieces[1].shape[1], local_heads, HDIM)
    newest = jnp.maximum(best, jnp.max(logits, -1))
    raised = jnp.exp(logits - newest[..., None])
    total = jnp.sum(raised, -1)
    accum = jnp.einsum(
        "shqk,skhd->sqhd",
        raised.astype(jnp.bfloat16),
        value_heads,
        preferred_element_type=jnp.float32,
    )
    best, total, accum = (newest, total, accum)
    log_total = best + jnp.log(total)
    attended = accum / jnp.transpose(total, (0, 2, 1))[..., None]
    attended_low = attended.reshape(seqs_here, span, local_heads * HDIM).astype(jnp.bfloat16)
    attn_rows = lax.all_to_all(attended_low, "seq", split_axis=1, concat_axis=2, tiled=True)
    attn_flat = attn_rows.reshape(flat_rows, width)
    projected = jnp.dot(attn_flat, gathered_output, preferred_element_type=jnp.float32).reshape(
        seqs_here, row_count, width
    )
    middle = source + gate_attn * projected
    mlp_in = adapt(middle, gain_second, shift_mlp, scale_mlp)
    mlp_low = mlp_in.astype(jnp.bfloat16).reshape(flat_rows, width)
    pre_act = jnp.dot(mlp_low, full_in, preferred_element_type=jnp.float32) + full_bias_in.astype(
        jnp.float32
    )
    active = gelu_tanh(pre_act).astype(jnp.bfloat16)
    branch = (
        jnp.dot(active, full_down, preferred_element_type=jnp.float32)
        + full_bias_down.astype(jnp.float32)
    ).reshape(seqs_here, row_count, width)
    output = (middle + gate_mlp * branch).astype(jnp.bfloat16)
    grad_result = cotangent.astype(jnp.float32)
    grad_gate_mlp = jnp.sum(grad_result * branch, 1, keepdims=True)
    grad_branch = (gate_mlp * grad_result).astype(jnp.bfloat16).reshape(flat_rows, width)
    grad_bias_down = jnp.sum(grad_branch.astype(jnp.float32), 0)
    grad_down = contract_rows(active, grad_branch)
    grad_active = contract_cols(grad_branch, full_down)
    unused_gelu, gelu_back = jax.vjp(gelu_tanh, pre_act)
    grad_pre = gelu_back(grad_active)[0].astype(jnp.bfloat16)
    grad_bias_in = jnp.sum(grad_pre.astype(jnp.float32), 0)
    grad_in = contract_rows(mlp_low, grad_pre)
    grad_mlp_in = contract_cols(grad_pre, full_in).reshape(seqs_here, row_count, width)
    unused_second, second_back = jax.vjp(adapt, middle, gain_second, shift_mlp, scale_mlp)
    grad_middle_norm, grad_gain_mlp, grad_shift_mlp, grad_scale_mlp = second_back(grad_mlp_in)
    grad_middle = grad_result + grad_middle_norm
    grad_gate_attn = jnp.sum(grad_middle * projected, 1, keepdims=True)
    grad_proj = (gate_attn * grad_middle).astype(jnp.bfloat16).reshape(flat_rows, width)
    grad_attn_weight = contract_rows(attn_flat, grad_proj)
    grad_attn_rows = (
        contract_cols(grad_proj, gathered_output)
        .astype(jnp.bfloat16)
        .reshape(seqs_here, row_count, width)
    )
    grad_heads = lax.all_to_all(grad_attn_rows, "seq", split_axis=2, concat_axis=1, tiled=True)
    grad_head_parts = grad_heads.reshape(seqs_here, span, local_heads, HDIM)
    delta = jnp.transpose(jnp.sum(grad_head_parts.astype(jnp.float32) * attended, -1), (0, 2, 1))
    pieces = (
        lax.all_gather(keys, "fsdp", axis=1, tiled=True),
        lax.all_gather(values, "fsdp", axis=1, tiled=True),
    )
    logits, key_heads = score_block(pieces[0])
    piece_rows = pieces[1].shape[1]
    value_heads = pieces[1].reshape(seqs_here, piece_rows, local_heads, HDIM)
    probs = jnp.exp(logits - log_total[..., None])
    grad_weights = jnp.einsum(
        "sqhd,skhd->shqk", grad_head_parts, value_heads, preferred_element_type=jnp.float32
    )
    probs, grad_logits = (probs, (probs * (grad_weights - delta[..., None])).astype(jnp.bfloat16))
    grad_query = (
        jnp.einsum("shqk,skhd->sqhd", grad_logits, key_heads, preferred_element_type=jnp.float32)
        * scale
    )
    key_part = (
        jnp.einsum("shqk,sqhd->skhd", grad_logits, query_heads, preferred_element_type=jnp.float32)
        * scale
    )
    value_part = jnp.einsum(
        "shqk,sqhd->skhd",
        probs.astype(jnp.bfloat16),
        grad_head_parts,
        preferred_element_type=jnp.float32,
    )
    grad_key_all = key_part.reshape(seqs_here, piece_rows, local_heads * HDIM)
    grad_value_all = value_part.reshape(seqs_here, piece_rows, local_heads * HDIM)
    folded_rows = (grad_query, grad_key_all, grad_value_all)
    grad_query, grad_key_all, grad_value_all = folded_rows
    grad_keys, grad_values = (
        lax.psum_scatter(grad_key_all, "fsdp", scatter_dimension=1, tiled=True),
        lax.psum_scatter(grad_value_all, "fsdp", scatter_dimension=1, tiled=True),
    )
    grad_parts = (
        lax.all_to_all(
            grad_query.reshape(seqs_here, span, local_heads * HDIM).astype(jnp.bfloat16),
            "seq",
            split_axis=1,
            concat_axis=2,
            tiled=True,
        ),
        lax.all_to_all(
            grad_keys.astype(jnp.bfloat16), "seq", split_axis=1, concat_axis=2, tiled=True
        ),
        lax.all_to_all(
            grad_values.astype(jnp.bfloat16), "seq", split_axis=1, concat_axis=2, tiled=True
        ),
    )
    unused_turn, reverse_rotation = jax.vjp(turn_all, qkv)
    grad_qkv = (
        reverse_rotation(tuple((member.astype(jnp.float32) for member in grad_parts)))[0]
        .astype(jnp.bfloat16)
        .reshape(flat_rows, 3 * width)
    )
    grad_qkv_weight = contract_rows(attn_low, grad_qkv)
    grad_attn_in = contract_cols(grad_qkv, full_qkv).reshape(seqs_here, row_count, width)
    unused_first, first_back = jax.vjp(adapt, source, gain_first, shift_attn, scale_attn)
    grad_source_norm, grad_gain_attn, grad_shift_attn, grad_scale_attn = first_back(grad_attn_in)
    grad_hidden = grad_middle + grad_source_norm
    grad_mod = jnp.concatenate(
        [
            grad_shift_attn,
            grad_scale_attn,
            grad_gate_attn,
            grad_shift_mlp,
            grad_scale_mlp,
            grad_gate_mlp,
        ],
        -1,
    )[:, 0, :]
    grad_ada = jnp.dot(grad_mod.T, cond, precision=highest_precision)
    grad_bias_mod = jnp.sum(grad_mod, 0)
    summed = (
        lax.psum_scatter(grad_qkv_weight, "fsdp", scatter_dimension=0, tiled=True),
        lax.psum_scatter(grad_attn_weight, "fsdp", scatter_dimension=0, tiled=True),
        lax.psum_scatter(grad_in, "fsdp", scatter_dimension=0, tiled=True),
        lax.psum_scatter(grad_down, "fsdp", scatter_dimension=0, tiled=True),
        lax.psum_scatter(grad_ada, "fsdp", scatter_dimension=0, tiled=True),
        lax.psum_scatter(grad_bias_mod, "fsdp", scatter_dimension=0, tiled=True),
        lax.psum_scatter(grad_gain_attn, "fsdp", scatter_dimension=0, tiled=True),
        lax.psum_scatter(grad_gain_mlp, "fsdp", scatter_dimension=0, tiled=True),
        lax.psum_scatter(grad_bias_in, "fsdp", scatter_dimension=0, tiled=True),
        lax.psum_scatter(grad_bias_down, "fsdp", scatter_dimension=0, tiled=True),
    )
    totals = (
        lax.psum(summed[0].astype(jnp.bfloat16), "seq").astype(jnp.float32),
        lax.psum(summed[1].astype(jnp.bfloat16), "seq").astype(jnp.float32),
        lax.psum(summed[2].astype(jnp.bfloat16), "seq").astype(jnp.float32),
        lax.psum(summed[3].astype(jnp.bfloat16), "seq").astype(jnp.float32),
        lax.psum(summed[4].astype(jnp.bfloat16), "seq").astype(jnp.float32),
        lax.psum(summed[5].astype(jnp.bfloat16), "seq").astype(jnp.float32),
        lax.psum(summed[6].astype(jnp.bfloat16), "seq").astype(jnp.float32),
        lax.psum(summed[7].astype(jnp.bfloat16), "seq").astype(jnp.float32),
        lax.psum(summed[8].astype(jnp.bfloat16), "seq").astype(jnp.float32),
        lax.psum(summed[9].astype(jnp.bfloat16), "seq").astype(jnp.float32),
    )
    return (output, grad_hidden) + tuple(totals)


AXES = ("seq", "fsdp")
SEQ_BIT, HALF_BIT, LOW_BIT, ROW_BIT, CORE_BIT = 16, 8, 4, 2, 1
STREAM = ((ROW_BIT, SEQ_BIT), (LOW_BIT, ROW_BIT), (SEQ_BIT, LOW_BIT))
TOKENS = ((LOW_BIT, LOW_BIT), (ROW_BIT, SEQ_BIT), (SEQ_BIT, ROW_BIT))
SHARED = ((LOW_BIT, LOW_BIT), (SEQ_BIT, SEQ_BIT), (ROW_BIT, ROW_BIT))
VMEM_LIMIT = 62 * 1024 * 1024


def swap_bits(values, even, odd=None):
    odd = even if odd is None else odd
    return lax.ppermute(values, AXES, [(i, i ^ (odd if i & 1 else even)) for i in range(32)])


def spread(values, order):
    for even, odd in order:
        values = jnp.concatenate([values, swap_bits(values, even, odd)], 0)
    return values


def collect(arrays, order):
    for even, odd in reversed(order):
        half = arrays[0].shape[0] // 2
        sent = jnp.concatenate([member[half:] for member in arrays], 1) if len(arrays) > 1 else arrays[0][half:]
        came = swap_bits(sent, even, odd)
        begin, summed = 0, []
        for member in arrays:
            part = came[:, begin : begin + member.shape[1]]
            begin += member.shape[1]
            summed.append((member[:half].astype(jnp.float32) + part.astype(jnp.float32)).astype(jnp.bfloat16))
        arrays = summed
    return arrays


def slot_masks(order, core):
    masks = [jnp.int32(0)]
    for even, odd in order:
        step = jnp.where(core == 0, even, odd).astype(jnp.int32)
        masks = masks + [mask ^ step for mask in masks]
    return jnp.stack(masks)


def quad_exchange(parts):
    came = swap_bits(parts[:, 1], ROW_BIT)
    parts = jnp.stack([parts[:, 0], came], 1)
    came = swap_bits(parts[1], LOW_BIT)
    return jnp.stack([parts[0], came], 0)


def after(values, *others):
    return lax.optimization_barrier((values,) + others)[0]


def pick(values, index, axis=0):
    return lax.dynamic_index_in_dim(values, index, axis, keepdims=False)


def pair_up(mine, other, position):
    return jnp.where(position == 0, jnp.stack([mine, other]), jnp.stack([other, mine]))


def dot_nn(left, right):
    return lax.dot_general(left, right, (((1,), (0,)), ((), ())), preferred_element_type=jnp.float32)


def row_norm(values):
    center = values - jnp.mean(values, -1, keepdims=True)
    return center * lax.rsqrt(jnp.mean(center * center, -1, keepdims=True) + 1e-05)


def head_select(width, head):
    lane = lax.broadcasted_iota(jnp.int32, (1, width), 1)
    return (lane % 128) // 32 == head


def vector_kernel(meta, cond, w_ada, bias_ada, gain_attn, gain_mlp, bias_in, bias_down, out):
    part = contract_cols(cond[...], w_ada[...])
    rest = part[0:2] + part[2:4] + part[4:6] + bias_ada[...].astype(jnp.float32)
    out[...] = jnp.zeros(out.shape, jnp.bfloat16)
    for row in range(3):
        rounded = rest.astype(jnp.bfloat16)
        rest = rest - rounded.astype(jnp.float32)
        out[row : row + 1, 0 : rest.shape[1]] = rounded[0:1]
        out[row + 3 : row + 4, 0 : rest.shape[1]] = rounded[1:2]
    for row, member in enumerate((gain_attn, gain_mlp, bias_in, bias_down)):
        out[6 + row : 7 + row, 0 : member.shape[1]] = member[...]


def share_kernel(meta, w_in, w_out, w_down, own, sent):
    core, side = meta[0], meta[1]
    lane = lax.broadcasted_iota(jnp.int32, (768, 384), 1)
    source = lax.broadcasted_iota(jnp.int32, (768, 384), 0)
    for target, which in ((own, core), (sent, 1 - core)):
        wanted = jnp.where(lane < 192, lane, lane + 192) + which * 192
        chosen = (source == wanted).astype(jnp.float32).astype(jnp.bfloat16)
        for i in range(4):
            target[i * 48 : (i + 1) * 48, :] = dot_nn(w_in[:, i * 768 : (i + 1) * 768], chosen).astype(jnp.bfloat16)
        target[192:240, :] = w_out[:, pl.ds(pl.multiple_of(which * 384, 128), 384)]
    rows = pl.ds(pl.multiple_of(side * 96, 32), 96)
    own[240:336, :] = w_down[rows, 0:384]
    own[336:432, :] = w_down[rows, 384:768]


def finish_kernel(meta, kept, came, source, grad_middle, vectors, stays, leaves):
    grad = kept[...].astype(jnp.float32) + came[...].astype(jnp.float32)
    center = source[...].astype(jnp.float32)
    center = center - jnp.mean(center, -1, keepdims=True)
    inverse = lax.rsqrt(jnp.mean(center * center, -1, keepdims=True) + 1e-05)
    norm = center * inverse
    scaled = grad * vectors[1:2, :] * vectors[0:1, :]
    result = grad_middle[...] + inverse * (
        scaled - jnp.mean(scaled, -1, keepdims=True) - norm * jnp.mean(scaled * norm, -1, keepdims=True)
    )
    half_way = stays.shape[0]
    stays[...] = result[:half_way]
    leaves[...] = result[half_way:].astype(jnp.bfloat16)


def order_weight_kernel(meta, own, other, chooser, out, gathered):
    for slot in range(16):
        start = pl.multiple_of(meta[48 + slot] * 48, 16)
        first = (slot % 8) * 48
        gathered[pl.ds(start, 48), :] = (own if slot < 8 else other)[first : first + 48, :]
    out[...] = dot_nn(gathered[...], chooser[...]).astype(jnp.bfloat16)


def project_kernel(
    meta, near, far, other_near, other_far, weight, vectors, cosine, sine, query_out, key_out, value_out, norm_out, all_queries
):
    step = pl.program_id(0)
    rows = near.shape[0]

    def project(source):
        norm = row_norm(source[...].astype(jnp.float32))
        norm_out[...] = norm.astype(jnp.bfloat16)
        attn_in = (norm * vectors[8:9, :] + vectors[2:3, :]).astype(jnp.bfloat16)
        packed = dot_nn(attn_in, weight[:, 256:768])
        first, second = packed[:, 0:128], packed[:, 128:256]
        turn_c, turn_s = cosine[...], sine[...]
        key_out[:, 0:128] = (first * turn_c - second * turn_s).astype(jnp.bfloat16)
        key_out[:, 128:256] = (second * turn_c + first * turn_s).astype(jnp.bfloat16)
        value_out[...] = packed[:, 256:512].astype(jnp.bfloat16)
        return attn_in

    def project_queries(attn_in):
        packed = dot_nn(attn_in, weight[:, 0:256]) * (HDIM ** (-0.5))
        first, second = packed[:, 0:128], packed[:, 128:256]
        turn_c, turn_s = cosine[...], sine[...]
        here = pl.ds(pl.multiple_of(step * rows, 256), rows)
        all_queries[here, 0:128] = (first * turn_c - second * turn_s).astype(jnp.bfloat16)
        all_queries[here, 128:256] = (second * turn_c + first * turn_s).astype(jnp.bfloat16)

    for number, source in enumerate((near, far, other_near, other_far)):

        @pl.when(step // 2 == number)
        def _(number=number, source=source):
            attn_in = project(source)
            if number < 2:
                project_queries(attn_in)

    @pl.when(step == 3)
    def _():
        block = query_out.shape[0] // 4
        stride = 1 + meta[64]
        for j in range(4):
            chosen = pl.ds(pl.multiple_of(((j >> 1) + (j & 1) * 2 * stride) * block, 128), block)
            query_out[j * block : (j + 1) * block, :] = all_queries[chosen, :]


def attend_kernel(meta, query_in, key_in, value_in, out_turned, log_out, out, value_turned):
    block = query_in.shape[0] // 4
    keys = key_in[...]
    value_turned[...] = value_in[...].T
    log_out[...] = jnp.zeros(log_out.shape, jnp.float32)
    out_turned[...] = jnp.zeros(out_turned.shape, jnp.float32)

    def body(number, carry):
        head = number % 3
        here = pl.ds(pl.multiple_of(number // 3 * 256, 256), 256)
        of_head = pl.ds(pl.multiple_of(head * 64, 64), 64)
        query = query_in[here, :]
        query = jnp.where(head_select(256, head), query, jnp.zeros_like(query))
        scores = contract_cols(keys, query)
        best = jnp.max(scores, 0, keepdims=True)
        raised = jnp.exp(scores - best)
        total = jnp.sum(raised, 0, keepdims=True)
        mixed = dot_nn(value_turned[of_head, :], raised.astype(jnp.bfloat16))
        out_turned[of_head, here] = mixed / total
        log_out[pl.ds(head, 1), here] = best + jnp.log(total)
        return carry

    lax.fori_loop(0, 3 * 4 * block // 256, body, 0)
    turned_back = out_turned[...].T.astype(jnp.bfloat16)
    for j in range(4):
        out[j, :, :] = turned_back[j * block : (j + 1) * block, 0:192]


def attend_back_kernel(
    meta, cosine, sine, query_in, key_in, value_in, out_turned, log_in, grad_in, grad_packed, key_sum, value_sum,
    product, grad_out, query_sums
):
    block = query_in.shape[0] // 4
    stride = 1 + meta[64]
    keys, values = key_in[...], value_in[...]
    key_turned = keys.T
    lane_pad = jnp.zeros((4 * block, 64), jnp.bfloat16)
    grad_out[...] = jnp.concatenate([jnp.concatenate([grad_in[j, :, :] for j in range(4)], 0), lane_pad], 1)
    key_sum[...] = jnp.zeros(key_sum.shape, jnp.float32)
    value_sum[...] = jnp.zeros(value_sum.shape, jnp.float32)
    product[...] = grad_out[...].astype(jnp.float32).T * out_turned[...]
    lane = lax.broadcasted_iota(jnp.int32, (1, 256), 1)

    def body(number, carry):
        head = number % 3
        here = pl.ds(pl.multiple_of(number // 3 * 256, 256), 256)
        query = query_in[here, :]
        query = jnp.where(head_select(256, head), query, jnp.zeros_like(query))
        head_grad = grad_out[here, :]
        head_grad = jnp.where(lane // 64 == head, head_grad, jnp.zeros_like(head_grad))
        probs = jnp.exp(contract_cols(keys, query) - log_in[pl.ds(head, 1), here])
        delta = jnp.sum(product[pl.ds(pl.multiple_of(head * 64, 64), 64), here], 0, keepdims=True)
        grad_scores = (probs * (contract_cols(values, head_grad) - delta)).astype(jnp.bfloat16)
        value_sum[...] += dot_nn(probs.astype(jnp.bfloat16), head_grad)
        key_sum[...] += dot_nn(grad_scores, query)
        part = dot_nn(key_turned, grad_scores).T * (HDIM ** (-0.5))
        query_sums[here, :] = jnp.where(head_select(256, head), part, query_sums[here, :])
        return carry

    query_sums[...] = jnp.zeros(query_sums.shape, jnp.float32)
    lax.fori_loop(0, 3 * 4 * block // 256, body, 0)
    for j in range(4):
        rows = pl.ds(pl.multiple_of(((j >> 1) + (j & 1) * 2 * stride) * block, 128), block)
        q_part = query_sums[j * block : (j + 1) * block, :]
        first, second = q_part[:, 0:128], q_part[:, 128:256]
        turn_c, turn_s = cosine[rows, :], sine[rows, :]
        here = slice(j * block, (j + 1) * block)
        grad_packed[here, 0:128] = (first * turn_c + second * turn_s).astype(jnp.bfloat16)
        grad_packed[here, 128:256] = (second * turn_c - first * turn_s).astype(jnp.bfloat16)


def project_back_kernel(
    meta, norm, weight, chooser, columns, cosine, sine, grad_packed, key_sum, value_sum,
    own_rows, other_rows, grad_weight, sums, grad_queries, weight_sum, total
):
    step = pl.program_id(0)
    rows = norm.shape[0]

    @pl.when(step == 0)
    def _():
        block = grad_packed.shape[0] // 4
        stride = 1 + meta[64]
        grad_queries[...] = jnp.zeros(grad_queries.shape, jnp.bfloat16)
        for j in range(4):
            chosen = pl.ds(pl.multiple_of(((j >> 1) + (j & 1) * 2 * stride) * block, 128), block)
            grad_queries[chosen, :] = grad_packed[j * block : (j + 1) * block, :]
        weight_sum[...] = jnp.zeros(weight_sum.shape, jnp.float32)
        total[...] = jnp.zeros(total.shape, jnp.float32)

    first, second = key_sum[:, 0:128], key_sum[:, 128:256]
    turn_c, turn_s = cosine[...], sine[...]
    pair = jnp.concatenate(
        [first * turn_c + second * turn_s, second * turn_c - first * turn_s, value_sum[...]], 1
    ).astype(jnp.bfloat16)
    ones = jnp.ones((8, rows), jnp.bfloat16)

    @pl.when(step < 4)
    def _():
        query = grad_queries[pl.ds(pl.multiple_of(step * rows, 256), rows), :]
        triple = jnp.concatenate([query, pair], 1)
        own_rows[...] = contract_cols(triple, weight[...]).astype(jnp.bfloat16)
        weight_sum[...] += contract_rows(norm[...], triple)
        total[...] += dot_nn(ones, triple)

    @pl.when(step >= 4)
    def _():
        other_rows[...] = contract_cols(pair, weight[:, 256:768]).astype(jnp.bfloat16)
        weight_sum[:, 256:768] += contract_rows(norm[...], pair)
        total[:, 256:768] += dot_nn(ones, pair)

    @pl.when(step == pl.num_programs(0) - 1)
    def _():
        summed = total[0:1, :]
        whole = columns[:, 0:1] * weight_sum[...] + columns[:, 1:2] * summed
        grad_weight[...] = contract_cols(whole.astype(jnp.bfloat16), chooser[...]).astype(jnp.bfloat16)
        plain = weight[...].astype(jnp.float32)
        sums[:, 0:1] = jnp.sum(plain * summed, 1, keepdims=True)
        sums[:, 1:2] = jnp.sum(plain * weight_sum[...], 1, keepdims=True)


def middle_kernel(
    meta, attended, near_a, near_b, far_a, far_b, other_near, other_far, own_rows, vectors, projected_out, middle_out, low_out,
    weight_out
):
    core = meta[64]
    mine = pl.multiple_of(core * 384, 128)
    theirs = pl.multiple_of(384 - core * 384, 128)
    for slot in range(16):
        rows_a = pl.ds(pl.multiple_of(meta[slot] * 48, 16), 48)
        rows_b = pl.ds(pl.multiple_of(meta[16 + slot] * 48, 16), 48)
        rows_p = pl.ds(pl.multiple_of(meta[32 + slot] * 48, 16), 48)
        part_a, part_b, other = (near_a, near_b, other_near) if slot < 8 else (far_a, far_b, other_far)
        weight_out[rows_a, pl.ds(mine, 256)] = part_a[slot % 8, :, :]
        weight_out[rows_b, pl.ds(pl.multiple_of(mine + 256, 128), 128)] = part_b[slot % 8, :, :]
        weight_out[rows_p, pl.ds(theirs, 256)] = other[slot % 8, :, 0:256]
        weight_out[rows_b, pl.ds(pl.multiple_of(theirs + 256, 128), 128)] = other[slot % 8, :, 256:384]
    projected = dot_nn(attended[...], weight_out[...])
    projected_out[...] = projected
    middle = own_rows[...].astype(jnp.float32) + vectors[3:4, :] * projected
    middle_out[...] = middle
    low_out[...] = (row_norm(middle) * vectors[4:5, :] * vectors[5:6, :] + vectors[6:7, :]).astype(jnp.bfloat16)


def mlp_kernel(
    meta, low_own, low_other, grad_own, grad_other, near_a, near_b, far_a, far_b, bias, sums_own, sums_other,
    keep_a, keep_b, send_a, send_b, grad_bias, weight_in, weight_down, grad_in, grad_down, branch, back
):
    def each_piece(base, part_a, part_b, move):
        def body(slot, carry):
            places = (0, 256, part_a, meta[base + slot]), (256, 128, part_b, meta[base + slot + 16])
            for lane_start, size, part, index in places:
                rows = pl.ds(pl.multiple_of(index * 48, 16), 48)
                for i in range(4):
                    lanes = slice(i * 384 + lane_start, i * 384 + lane_start + size)
                    move(part, (slot, pl.ds(i * 48, 48)), False, (rows, lanes))
                rows = pl.ds(pl.multiple_of(index * 96, 16), 96)
                for i in range(2):
                    lanes = slice(i * 384 + lane_start, i * 384 + lane_start + size)
                    move(part, (slot, pl.ds(192 + i * 96, 96)), True, (rows, lanes))
            return carry

        lax.fori_loop(0, 8, body, 0)

    def gather(part, piece, down, place):
        (weight_down if down else weight_in)[place] = part[piece]

    def scatter(part, piece, down, place):
        part[piece] = (grad_down if down else grad_in)[place]

    each_piece(0, near_a, near_b, gather)
    each_piece(8, far_a, far_b, gather)
    low = jnp.concatenate([low_own[...], low_other[...]], 0)
    grad = jnp.concatenate([grad_own[...], grad_other[...]], 0)
    tokens = low_own.shape[0]
    branch[...] = jnp.zeros(branch.shape, jnp.float32)
    back[...] = jnp.zeros(back.shape, jnp.float32)
    root, cubic = math.sqrt(2.0 / math.pi), 0.044715

    def body(number, carry):
        hidden = pl.ds(pl.multiple_of(number * 384, 128), 384)
        pre_act = dot_nn(low, weight_in[:, hidden]) + bias[:, hidden]
        square = pre_act * pre_act
        bend = jnp.tanh(root * (pre_act + cubic * square * pre_act))
        active = (0.5 * pre_act * (1.0 + bend)).astype(jnp.bfloat16)
        slope = 0.5 * (1.0 + bend) + 0.5 * pre_act * (1.0 - bend * bend) * (root * (1.0 + 3.0 * cubic * square))
        branch[...] += dot_nn(active, weight_down[hidden, :])
        grad_pre = (contract_cols(grad, weight_down[hidden, :]) * slope).astype(jnp.bfloat16)
        grad_bias[:, hidden] = jnp.sum(grad_pre.astype(jnp.float32), 0, keepdims=True)
        back[...] += contract_cols(grad_pre, weight_in[:, hidden])
        grad_in[:, hidden] = contract_rows(low, grad_pre).astype(jnp.bfloat16)
        grad_down[hidden, :] = contract_rows(active, grad).astype(jnp.bfloat16)
        return carry

    lax.fori_loop(0, 4, body, 0)
    sums_own[0, :, :] = branch[:tokens, :]
    sums_other[0, :, :] = branch[tokens:, :]
    sums_own[1, :, :] = back[:tokens, :]
    sums_other[1, :, :] = back[tokens:, :]
    each_piece(0, keep_a, keep_b, scatter)
    each_piece(8, send_a, send_b, scatter)


def turn_kernel(
    meta, sums_own, sums_other, bias, middle_in, projected_in, cotangent, grad_branch, weight,
    attended, vectors, output, grad_middle_out, grad_attn_out, grad_weight, sums
):
    width = middle_in.shape[1]
    branch = sums_own[0, :, :] + sums_other[0, :, :] + bias[...]
    middle = middle_in[...]
    grad = cotangent[...].astype(jnp.float32)
    output[...] = (middle + vectors[7:8, :] * branch).astype(jnp.bfloat16)
    back = sums_own[1, :, :] + sums_other[1, :, :]
    center = middle - jnp.mean(middle, -1, keepdims=True)
    inverse = lax.rsqrt(jnp.mean(center * center, -1, keepdims=True) + 1e-05)
    norm = center * inverse
    scaled = back * vectors[5:6, :] * vectors[4:5, :]
    grad_middle = grad + inverse * (
        scaled - jnp.mean(scaled, -1, keepdims=True) - norm * jnp.mean(scaled * norm, -1, keepdims=True)
    )
    grad_middle_out[...] = grad_middle
    grad_proj = (vectors[3:4, :] * grad_middle).astype(jnp.bfloat16)
    grad_attn_out[...] = contract_cols(grad_proj, weight[...]).astype(jnp.bfloat16)
    grad_weight[...] = contract_rows(attended[...], grad_proj).astype(jnp.bfloat16)
    def total(values):
        return jnp.sum(values, 0, keepdims=True)

    sums[...] = jnp.concatenate(
        [
            total(grad_middle * projected_in[...]),
            total(back),
            total(back * norm),
            total(grad * branch),
            total(grad_branch[...].astype(jnp.float32)),
            jnp.zeros((3, width), jnp.float32),
        ],
        0,
    )


def call(body, outs, args, scratch=(), grid=None, blocks=(), out_blocks=(), flops=0, moved=0):
    if grid is None:
        whole = pl.BlockSpec(memory_space=pltpu.VMEM)
        in_specs, out_specs = [whole] * len(args), [whole] * len(outs)
    else:
        blocks, out_blocks = dict(blocks), dict(out_blocks)

        def spec(shape, block):
            return block or pl.BlockSpec(shape, lambda i: (0,) * len(shape))

        in_specs = [spec(member.shape, blocks.get(k)) for k, member in enumerate(args)]
        out_specs = [spec(member[0], out_blocks.get(k)) for k, member in enumerate(outs)]
    in_specs[0] = pl.BlockSpec(memory_space=pltpu.SMEM)
    return pl.pallas_call(
        body,
        grid=() if grid is None else grid,
        out_shape=[jax.ShapeDtypeStruct(*member) for member in outs],
        in_specs=in_specs,
        out_specs=out_specs,
        scratch_shapes=[pltpu.VMEM(*member) for member in scratch],
        compiler_params=pltpu.CompilerParams(vmem_limit_bytes=VMEM_LIMIT),
        cost_estimate=pl.CostEstimate(flops=flops, bytes_accessed=moved, transcendentals=0),
    )(*args)


def cube_local(
    hidden_in, time_index, cotangent, w_qkv, w_attn_out, w_mlp_in, w_mlp_out, w_ada, bias_ada, gain_attn, gain_mlp,
    bias_mlp_in, bias_mlp_out
):
    f32, bf16 = jnp.float32, jnp.bfloat16
    rows, width = hidden_in.shape[1:]
    tokens = 2 * rows
    place = lax.axis_index("fsdp")
    side = lax.axis_index("seq")
    device = side * 16 + place
    core, half, group = place & 1, place >> 3, (place >> 1) & 3
    x_own = jnp.concatenate(
        [pick(hidden_in, half), swap_bits(pick(hidden_in, 1 - half), HALF_BIT)], 0
    )
    cond = jax.nn.silu(time_features(time_index, w_ada.shape[1]))
    cond_parts, rest = [], cond
    for _ in range(3):
        cond_parts.append(lax.reduce_precision(rest, 8, 7))
        rest = rest - cond_parts[-1]
    cond_parts = jnp.concatenate(cond_parts + [jnp.zeros_like(cond)], 0).astype(bf16)

    def double(values, bit):
        return jnp.concatenate([values, swap_bits(values, bit)], 0)

    (vector,) = call(
        vector_kernel,
        [((16, 576), bf16)],
        [jnp.zeros((1,), jnp.int32), cond_parts, w_ada]
        + [member[None] for member in (bias_ada, gain_attn, gain_mlp, bias_mlp_in, bias_mlp_out)],
    )
    grouped = w_qkv.reshape(48, 3, 4, 192).transpose(2, 0, 1, 3).reshape(4, 48, 576)
    grouped = grouped[group ^ jnp.arange(4)].reshape(192, 576)
    grouped = jnp.concatenate([grouped, vector], 0)
    x_own, grouped, w_mlp_in, w_attn_out, w_mlp_out = lax.optimization_barrier(
        (x_own, grouped, w_mlp_in, w_attn_out, w_mlp_out)
    )
    x_kept = x_own
    x_one = spread(x_own, TOKENS[:1])
    came_qkv = swap_bits(grouped, HALF_BIT)
    own_share, sent_share = call(
        share_kernel,
        [((432, 384), bf16), ((240, 384), bf16)],
        [jnp.stack([core, side]).astype(jnp.int32), w_mlp_in, w_attn_out, w_mlp_out],
    )
    came_share = swap_bits(sent_share, CORE_BIT)
    share = jnp.where(core == side, own_share[:240], came_share)
    share = jnp.concatenate([share[:192], own_share[240:], share[192:]], 0)
    x_one, share, place_kept = lax.optimization_barrier((x_one, share, place))
    x_two = spread(x_one, TOKENS[1:2])
    came_share = swap_bits(share, HALF_BIT)
    place = place_kept
    device, core = side * 16 + place, place & 1
    stream_own, stream_other = slot_masks(STREAM, core), slot_masks(STREAM, 1 - core)
    shared = slot_masks(SHARED, core)

    def weight_slots(masks):
        moved = ((masks & 6) | (masks >> 4))[:, None] ^ jnp.array([0, 8], jnp.int32)[None]
        return (((place & 14) + side) ^ moved).reshape(-1)

    quad = jnp.array([0, ROW_BIT, LOW_BIT, LOW_BIT | ROW_BIT], jnp.int32)
    oct_masks = (quad[:, None] ^ jnp.array([0, HALF_BIT], jnp.int32)).reshape(-1)
    row_slots = place ^ jnp.concatenate([oct_masks, oct_masks ^ CORE_BIT])
    meta = jnp.concatenate(
        [weight_slots(stream_own), weight_slots(shared), weight_slots(stream_other), row_slots, core[None]]
    ).astype(jnp.int32)
    blocks = jnp.concatenate(
        [device ^ slot_masks(TOKENS, core), device ^ CORE_BIT ^ slot_masks(TOKENS, 1 - core)]
    )
    blocks = jnp.stack([blocks, blocks ^ HALF_BIT], 1)
    inverse = jnp.exp(-math.log(10000.0) * (2 * (jnp.arange(128) % 32)).astype(f32) / HDIM)
    begin_angles = (blocks.reshape(-1) * rows).astype(f32)[:, None, None] * inverse
    inner_angles = jnp.arange(rows, dtype=jnp.int32).astype(f32)[:, None] * inverse
    begin_c, begin_s, inner_c, inner_s = [
        lax.optimization_barrier(member)
        for member in (jnp.cos(begin_angles), jnp.sin(begin_angles), jnp.cos(inner_angles), jnp.sin(inner_angles))
    ]
    cosine = (begin_c * inner_c - begin_s * inner_s).reshape(-1, 128)
    sine = (begin_s * inner_c + begin_c * inner_s).reshape(-1, 128)
    lane = jnp.arange(768) + (place >> 4)
    inner = lane % 128
    wanted = jnp.where(
        lane < 512,
        jnp.where(inner < 96, (lane // 256) * 192 + (inner // 32) * 64 + ((lane % 256) // 128) * 32 + inner % 32, -1),
        jnp.where(lane < 704, lane - 128, -1),
    )
    chooser = (jnp.arange(576)[:, None] == wanted[None, :]).astype(bf16)
    x_two, grouped, came_qkv, meta, cosine, sine, chooser = lax.optimization_barrier(
        (x_two, grouped, came_qkv, meta, cosine, sine, chooser)
    )
    x_far = swap_bits(x_two, *TOKENS[2])
    other_two = swap_bits(x_two, CORE_BIT)
    both_qkv = jnp.stack([grouped[:192], came_qkv[:192]]).reshape(2, 2, 2, 48, 576)
    vector = jnp.concatenate([grouped[192:], came_qkv[192:]], 0)
    got = swap_bits(jnp.concatenate([both_qkv[:, :, 1].reshape(192, 576), vector], 0), ROW_BIT)
    got, came_share, cotangent = lax.optimization_barrier((got, came_share, cotangent))
    both_qkv = jnp.stack([both_qkv[:, :, 0], got[:192].reshape(2, 2, 48, 576)])
    vector = jnp.concatenate([vector, got[192:]], 0)
    got = swap_bits(jnp.concatenate([both_qkv[:, :, 1].reshape(192, 576), vector], 0), LOW_BIT)
    share = jnp.stack([share, came_share])[None]
    part_a, part_b = spread(share[..., :256], STREAM[:1]), spread(share[..., 256:], SHARED[:1])
    x_far, got, part_a, part_b = lax.optimization_barrier((x_far, got, part_a, part_b))
    grouped = jnp.concatenate([both_qkv[:, :, 0].reshape(192, 576), got[:192], vector, got[192:]], 0)
    came_grouped = swap_bits(grouped, CORE_BIT)
    other_far = swap_bits(x_far, CORE_BIT)
    came_a, came_b = swap_bits(part_a, *STREAM[1]), swap_bits(part_b, *SHARED[1])
    apart = place ^ jnp.arange(16)
    vector = jnp.concatenate([grouped[384:], came_grouped[384:]], 0).reshape(16, 16, 576).astype(f32)
    vector = vector[((apart & 1) << 3) | (apart & 4) | (apart & 2) | (apart >> 3)]
    parts = [jnp.sum(vector[:, row : row + 3, :288], 1) for row in (0, 3)]
    parts += [vector[:, 6 + row, :size] for row, size in enumerate((48, 48, 192, 48))]
    modulation = jnp.stack([parts[0].reshape(6, width), parts[1].reshape(6, width)])
    shift_attn, scale_attn, gate_attn, shift_mlp, scale_mlp, gate_mlp = [
        row for row in pick(modulation, half)
    ]
    full_gain_attn, full_gain_mlp = parts[2].reshape(-1), parts[3].reshape(-1)
    bias_in = pick(parts[4].reshape(8, 2, 192), core, 1).reshape(1, -1)
    bias_down = parts[5].reshape(1, -1)
    vectors = jnp.stack(
        [full_gain_attn, 1.0 + scale_attn, shift_attn, gate_attn, full_gain_mlp, 1.0 + scale_mlp, shift_mlp, gate_mlp]
        + [full_gain_attn * (1.0 + scale_attn)]
    )
    columns = jnp.stack([vectors[8], shift_attn], 1)
    (weight_qkv,) = call(
        order_weight_kernel,
        [((768, 768), bf16)],
        [meta, grouped, came_grouped, chooser],
        [((768, 576), bf16)],
        flops=2 * 768 * 768 * 576,
        moved=3_000_000,
    )
    span = 16 * tokens
    chunk = 256

    def part_of(number, size):
        return pl.BlockSpec((chunk, size), lambda i: (jnp.clip(i - number * 2, 0, 1), 0))

    def rows_of(size):
        return pl.BlockSpec((chunk, size), lambda i: (i, 0))

    queries, keys, values, norms = call(
        project_kernel,
        [((4 * tokens, 256), bf16), ((span, 256), bf16), ((span, 256), bf16), ((span, width), bf16)],
        [meta, x_two, x_far, other_two, other_far, weight_qkv, vectors, cosine, sine],
        [((8 * tokens, 256), bf16)],
        grid=(8,),
        blocks=[(1 + number, part_of(number, width)) for number in range(4)] + [(7, rows_of(128)), (8, rows_of(128))],
        out_blocks=[(1, rows_of(256)), (2, rows_of(256)), (3, rows_of(width))],
        flops=2_000_000_000,
        moved=8_000_000,
    )
    keys, came_a, came_b = lax.optimization_barrier((keys, came_a, came_b))
    part_a, part_b = jnp.concatenate([part_a, came_a], 0), jnp.concatenate([part_b, came_b], 0)
    far_a, far_b = swap_bits(part_a, *STREAM[2]), swap_bits(part_b, *SHARED[2])
    part_a, part_b = part_a.reshape(8, 432, 256), part_b.reshape(8, 432, 128)
    other_near = swap_bits(jnp.concatenate([part_a[:, 384:], part_b[:, 384:]], 2), CORE_BIT)
    out_turned, log_total, heads_out = call(
        attend_kernel,
        [((256, 4 * tokens), f32), ((8, 4 * tokens), f32), ((4, tokens, 192), bf16)],
        [meta, queries, keys, values],
        [((256, span), bf16)],
        flops=8_000_000_000,
        moved=4_000_000,
    )
    heads_out = heads_out.reshape(2, 2, tokens, 192)
    came = swap_bits(heads_out[:, 1], ROW_BIT)
    came, far_a, far_b = lax.optimization_barrier((came, far_a, far_b))
    heads_out = jnp.stack([heads_out[:, 0], came], 1)
    by_group = jnp.stack([heads_out[0], swap_bits(heads_out[1], LOW_BIT)], 0).reshape(4, tokens, 192)
    attended = by_group[group ^ jnp.arange(4)].transpose(1, 0, 2).reshape(tokens, width)
    far_a, far_b = far_a.reshape(8, 432, 256), far_b.reshape(8, 432, 128)
    other_out = swap_bits(jnp.concatenate([far_a[:, 384:], far_b[:, 384:]], 2), CORE_BIT)
    projected, middle, mlp_own, weight_out = call(
        middle_kernel,
        [((tokens, width), f32), ((tokens, width), f32), ((tokens, width), bf16), ((768, 768), bf16)],
        [meta, attended, part_a[:, 384:], part_b[:, 384:], far_a[:, 384:], far_b[:, 384:], other_near, other_out]
        + [x_kept, vectors],
        flops=150_000_000,
        moved=3_000_000,
    )
    grad_own = jnp.concatenate(
        [pick(cotangent, half), swap_bits(pick(cotangent, 1 - half), HALF_BIT)], 0
    )
    branch_grad = (gate_mlp[None] * grad_own.astype(f32)).astype(bf16)
    branch_grad_other = swap_bits(branch_grad, CORE_BIT)
    mlp_other = swap_bits(mlp_own, CORE_BIT)
    sums_own, sums_sent, keep_a, keep_b, send_a, send_b, grad_bias_in = call(
        mlp_kernel,
        [((2, tokens, width), f32)] * 2
        + [((8, 384, 256), bf16), ((8, 384, 128), bf16)] * 2
        + [((1, 1536), f32)],
        [meta, mlp_own, mlp_other, branch_grad, branch_grad_other, part_a, part_b, far_a, far_b, bias_in],
        [((768, 1536), bf16), ((1536, 768), bf16), ((768, 1536), bf16), ((1536, 768), bf16)]
        + [((2 * tokens, width), f32)] * 2,
        flops=3_600_000_000,
        moved=12_000_000,
    )
    came = swap_bits(sums_sent, CORE_BIT)

    def plus(left, right):
        return (left.astype(f32) + right.astype(f32)).astype(bf16)

    came_a, came_b = swap_bits(send_a, *STREAM[2]), swap_bits(send_b, *SHARED[2])
    output_rows, grad_middle, grad_attn, grad_w_out, sums_mlp = call(
        turn_kernel,
        [((tokens, width), bf16), ((tokens, width), f32), ((tokens, width), bf16), ((768, 768), bf16), ((8, width), f32)],
        [meta, sums_own, came, bias_down, middle, projected, grad_own, branch_grad, weight_out]
        + [attended, vectors],
        flops=300_000_000,
        moved=5_000_000,
    )

    grad_heads = grad_attn.reshape(tokens, 4, 192).transpose(1, 0, 2)[group ^ jnp.arange(4)]
    grad_heads = quad_exchange(grad_heads.reshape(2, 2, tokens, 192)).reshape(4, tokens, 192)
    grad_heads, grad_w_out, output_rows = lax.optimization_barrier((grad_heads, grad_w_out, output_rows))
    by_core = grad_w_out.reshape(8, 2, 48, width)
    sum_out = plus(pick(by_core, core, 1), swap_bits(pick(by_core, 1 - core, 1), CORE_BIT))
    output = pair_up(output_rows[:rows], swap_bits(output_rows[rows:], HALF_BIT), half)
    grad_packed, key_sum, value_sum = call(
        attend_back_kernel,
        [((4 * tokens, 256), bf16), ((span, 256), f32), ((span, 256), f32)],
        [meta, cosine, sine, queries, keys, values, out_turned, log_total, grad_heads],
        [((256, 4 * tokens), f32), ((4 * tokens, 256), bf16), ((4 * tokens, 256), f32)],
        flops=14_000_000_000,
        moved=8_000_000,
    )
    key_sum, came_a, came_b, sum_out, output = lax.optimization_barrier((key_sum, came_a, came_b, sum_out, output))
    sum_a = plus(keep_a, came_a).reshape(4, 768, 256)
    sum_b = plus(keep_b, came_b).reshape(4, 768, 128)
    came_a, came_b = swap_bits(sum_a[2:], *STREAM[1]), swap_bits(sum_b[2:], *SHARED[1])
    y, z = (place >> 1) & 1, (place >> 2) & 1
    out_row = sum_out.reshape(2, 2, 2, 48, width)
    came_out = swap_bits(pick(out_row, 1 - y, 2), ROW_BIT)
    own_rows, other_rows, grad_qkv, sums_attn = call(
        project_back_kernel,
        [((8 * tokens, width), bf16)] * 2 + [((768, 576), bf16), ((width, 2), f32)],
        [meta, norms, weight_qkv, chooser, columns, cosine, sine, grad_packed, key_sum, value_sum],
        [((8 * tokens, 256), bf16), ((width, width), f32), ((8, width), f32)],
        grid=(8,),
        blocks=[(1, rows_of(width)), (5, rows_of(128)), (6, rows_of(128)), (8, rows_of(256)), (9, rows_of(256))],
        out_blocks=[
            (0, pl.BlockSpec((chunk, width), lambda i: (jnp.minimum(i, 3), 0))),
            (1, pl.BlockSpec((chunk, width), lambda i: (jnp.maximum(i - 4, 0), 0))),
        ],
        flops=6_000_000_000,
        moved=16_000_000,
    )
    own_rows, other_rows, grad_qkv, sums_attn, came_a, came_b, came_out = lax.optimization_barrier(
        (own_rows, other_rows, grad_qkv, sums_attn, came_a, came_b, came_out)
    )
    own_rows = own_rows.reshape(8, tokens, width)
    came_rows = swap_bits(other_rows, CORE_BIT).reshape(8, tokens, width)
    small = jnp.concatenate([sums_attn.T, sums_mlp[0:5]], 0)
    small = jnp.concatenate([small + swap_bits(small, CORE_BIT), grad_bias_in.reshape(2, width)], 0)
    by_core = grad_qkv.reshape(8, 2, 48, 576)
    kept = plus(pick(by_core, core, 1), swap_bits(pick(by_core, 1 - core, 1), CORE_BIT))
    sum_a, sum_b = plus(sum_a[:2], came_a), plus(sum_b[:2], came_b)
    sum_out = plus(pick(out_row, y, 2), came_out)
    came_a, came_b = swap_bits(sum_a[1], *STREAM[0]), swap_bits(sum_b[1], *SHARED[0])

    def sum_step(own, came, small, order):
        half_way = own.shape[0] // 2
        sent = plus(own[half_way:], came[half_way:]).reshape(-1, width)
        high = jnp.pad(small, ((0, 7), (0, 0))).astype(bf16)
        low = (jnp.pad(small, ((0, 7), (0, 0))) - high.astype(f32)).astype(bf16)
        got = swap_bits(jnp.concatenate([sent, high, low], 0), *order)
        count = sent.shape[0]
        small = small + got[count : count + 9].astype(f32) + got[count + 16 : count + 25].astype(f32)
        return plus(own[:half_way], came[:half_way]), got[:count].reshape(half_way, tokens, width), small

    came_rows, small, kept, came_a, came_b = lax.optimization_barrier((came_rows, small, kept, came_a, came_b))
    own_rows, came_rows, small = sum_step(own_rows, came_rows, small, TOKENS[2])

    def with_out(of_qkv, of_out):
        count = of_qkv.size // 576
        blocks = count * width // of_out.size
        of_out = of_out.reshape(-1, blocks, width // blocks).transpose(1, 0, 2).reshape(count, -1)
        return jnp.concatenate([of_qkv.reshape(count, 576), of_out], 1)

    def without(got, of_qkv, of_out):
        blocks = width // (got.shape[1] - 576)
        out = got[:, 576:].reshape(blocks, -1, width // blocks).transpose(1, 0, 2).reshape(of_out.shape)
        return got[:, :576].reshape(of_qkv.shape), out

    sum_a, sum_b = plus(sum_a[0], came_a).reshape(2, 384, 256), plus(sum_b[0], came_b).reshape(2, 384, 128)
    total = jnp.concatenate([sum_a, sum_b], 2)
    came_total = swap_bits(total[1], HALF_BIT)
    by_row = kept.reshape(2, 2, 2, 48, 576)
    by_row = jnp.stack([pick(by_row, y, 2), swap_bits(pick(by_row, 1 - y, 2), ROW_BIT)])
    came_rows, by_row, sum_out, small, came_total = lax.optimization_barrier(
        (came_rows, by_row, sum_out, small, came_total)
    )
    total = plus(total[0], came_total)
    across = swap_bits(total, SEQ_BIT)
    own_rows, came_rows, small = sum_step(own_rows, came_rows, small, TOKENS[1])
    sent = pick(by_row, 1 - z, 2), pick(sum_out, 1 - z, 1)
    got = without(swap_bits(with_out(*sent), LOW_BIT), *sent)
    kept, sum_out = jnp.stack([pick(by_row, z, 2), got[0]]), plus(pick(sum_out, z, 1), got[1])
    came_rows, kept, small, sum_out, across = lax.optimization_barrier((came_rows, kept, small, sum_out, across))
    mine = jnp.where(core == side, total[:192], across[:192])
    theirs = swap_bits(jnp.where(core == side, across[:192], total[:192]), CORE_BIT)
    own_rows, came_rows, small = sum_step(own_rows, came_rows, small, TOKENS[0])
    by_half = kept.reshape(4, 2, 48, 576)
    sent = pick(by_half, 1 - half, 1), pick(sum_out, 1 - half)
    got = without(swap_bits(with_out(*sent), HALF_BIT), *sent)
    kept, sum_out = plus(pick(by_half, half, 1), got[0]), plus(pick(sum_out, half), got[1])
    came_rows, small, theirs = lax.optimization_barrier((came_rows, small, theirs))
    stays, leaves = call(
        finish_kernel,
        [((rows, width), f32), ((rows, width), bf16)],
        [jnp.zeros((1,), jnp.int32), own_rows[0], came_rows[0], x_kept, grad_middle, vectors],
    )
    leaves_came = swap_bits(leaves, HALF_BIT)

    grad_down = pair_up(total[192:], across[192:], side).reshape(2, 2, 96, 384)
    grad_down = grad_down.transpose(0, 2, 1, 3).reshape(192, 768).astype(f32)
    def in_columns_back(blocks):
        return blocks.reshape(4, 48, 384).transpose(1, 0, 2).reshape(48, 8, 192)

    grad_w_in = pair_up(in_columns_back(mine), in_columns_back(theirs), core)
    grad_w_in = grad_w_in.transpose(1, 2, 0, 3).reshape(48, 3072).astype(f32)
    kept = kept[group ^ jnp.arange(4)].reshape(4, 48, 3, 192).transpose(1, 2, 0, 3).reshape(48, 2304)
    kept = jnp.concatenate([kept, sum_out], 1)
    kept, came_small, leaves_came = lax.optimization_barrier((kept, swap_bits(small, HALF_BIT), leaves_came))
    grad_hidden = pair_up(stays, leaves_came.astype(f32), half)
    came_kept = swap_bits(kept, SEQ_BIT)
    kept = kept.astype(f32) + came_kept.astype(f32)
    grad_w_qkv, grad_w_out = kept[:, :2304], kept[:, 2304:]
    both = pair_up(small, came_small, half)
    plus_scale = 1.0 + modulation[:, 1], 1.0 + modulation[:, 4]
    grad_mod = jnp.stack(
        [both[:, 0], both[:, 1] * full_gain_attn, both[:, 2], both[:, 3], both[:, 4] * full_gain_mlp, both[:, 5]], 1
    ).reshape(2, 16, 288)
    grad_mod = pick(grad_mod, place, 1)
    grad_ada = grad_mod[0][:, None] * cond[0][None] + grad_mod[1][:, None] * cond[1][None]
    gain_first = pick(jnp.sum(both[:, 1] * plus_scale[0], 0).reshape(16, 48), place)
    gain_second = pick(jnp.sum(both[:, 4] * plus_scale[1], 0).reshape(16, 48), place)
    summed = both[0] + both[1]
    bias_in_grad = pick(summed[7:9].reshape(8, 192), place >> 1)
    bias_down_grad = pick(summed[6].reshape(16, 48), place)
    return (
        output,
        grad_hidden,
        grad_w_qkv,
        grad_w_out,
        grad_w_in,
        grad_down,
        grad_ada,
        jnp.sum(grad_mod, 0),
        gain_first,
        gain_second,
        bias_in_grad,
        bias_down_grad,
    )


def solution(mesh):
    return jax.shard_map(
        cube_local if dict(mesh.shape) == {"seq": 2, "fsdp": 16} else local,
        mesh=mesh,
        in_specs=(
            P(None, ("seq", "fsdp"), None),
            P(),
            P(None, ("seq", "fsdp"), None),
            P("fsdp", None),
            P("fsdp", None),
            P("fsdp", None),
            P("fsdp", None),
            P("fsdp", None),
            P("fsdp"),
            P("fsdp"),
            P("fsdp"),
            P("fsdp"),
            P("fsdp"),
        ),
        out_specs=(
            P(None, ("seq", "fsdp"), None),
            P(None, ("seq", "fsdp"), None),
            P("fsdp", None),
            P("fsdp", None),
            P("fsdp", None),
            P("fsdp", None),
            P("fsdp", None),
            P("fsdp"),
            P("fsdp"),
            P("fsdp"),
            P("fsdp"),
            P("fsdp"),
        ),
        check_vma=False,
    )
```

profile of v0, /device:TPU:0, one launch (start us, length us, event | category | flops | bytes accessed | tf_op | source)
XLA Modules:
  0.0 303.5 jit_solution(11199185136134976368)
XLA Ops:
  1.6 4.1 %collective-permute-start = (bf16[64,768]{1,0:T(8,128)(2,1)S(1)}, bf16[64,768]{1,0:T(8,128)(2,1)S(1)}, u32[]{:S(2)}, u32[]{:S(2)}) collective-permute-start(bf16[64,768]{1,0:T(8,128)(2,1)S(1)} %get-tuple-element.263), channel_id=1, source_target_pairs={{0,8},{1,9},{2,10},{3,11},{4,12},{5,13},{6,14},{7,15},{8,0},{9,1},... | collective-permute-start | bytes 294920 | tf_op jit(solution)/shard_map/ppermute | solution.py:329
  12.6 1.7 shard_map.265
  15.6 2.6 shard_map.266
  18.3 1.6 collective-permute-start.1
  22.3 4.0 %collective-permute-done.1 = bf16[128,768]{1,0:T(8,128)(2,1)S(1)} collective-permute-done((bf16[128,768]{1,0:T(8,128)(2,1)S(1)}, bf16[128,768]{1,0:T(8,128)(2,1)S(1)}, u32[]{:S(2)}, u32[]{:S(2)}) %collective-permute-start.1) | collective-permute-done | bytes 196640 | tf_op jit(solution)/shard_map/ppermute | solution.py:329
  26.4 1.8 collective-permute-start.3
  30.5 2.8 collective-permute-start.7
  33.3 1.6 multiply_add_fusion
  36.6 7.0 %collective-permute-done.4 = bf16[208,576]{1,0:T(8,128)(2,1)S(1)} collective-permute-done((bf16[208,576]{1,0:T(8,128)(2,1)S(1)}, bf16[208,576]{1,0:T(8,128)(2,1)S(1)}, u32[]{:S(2)}, u32[]{:S(2)}) %collective-permute-start.4) | collective-permute-done | bytes 239648 | tf_op jit(solution)/shard_map/ppermute | solution.py:329
  43.8 1.6 collective-permute-start.6
  46.9 3.3 %collective-permute-done.7 = bf16[432,384]{1,0:T(8,128)(2,1)S(1)} collective-permute-done((bf16[432,384]{1,0:T(8,128)(2,1)S(1)}, bf16[432,384]{1,0:T(8,128)(2,1)S(1)}, u32[]{:S(2)}, u32[]{:S(2)}) %collective-permute-start.7) | collective-permute-done | bytes 331808 | tf_op jit(solution)/shard_map/ppermute | solution.py:329
  50.2 2.8 collective-permute-done.6
  54.9 2.1 collective-permute-start.8
  57.0 5.1 %collective-permute-done.10 = bf16[1,2,432,128]{3,2,1,0:T(8,128)(2,1)S(1)} collective-permute-done((bf16[1,2,432,128]{3,2,1,0:T(8,128)(2,1)S(1)}, bf16[1,2,432,128]{3,2,1,0:T(8,128)(2,1)S(1)}, u32[]{:S(2)}, u32[]{:S(2)}) %collective-permute-start.10) | collective-permute-done | bytes 221216 | tf_op jit(solution)/shard_map/ppermute | solution.py:329
  62.3 3.4 %collective-permute-done.8 = bf16[256,576]{1,0:T(8,128)(2,1)S(1)} collective-permute-done((bf16[256,576]{1,0:T(8,128)(2,1)S(1)}, bf16[256,576]{1,0:T(8,128)(2,1)S(1)}, u32[]{:S(2)}, u32[]{:S(2)}) %collective-permute-start.8) | collective-permute-done | bytes 294944 | tf_op jit(solution)/shard_map/ppermute | solution.py:329
  78.7 3.8 %shard_map.267.weight = bf16[768,768]{1,0:T(8,128)(2,1)} custom-call(s32[65]{0:T(128)} %concatenate.150.meta, bf16[512,576]{1,0:T(8,128)(2,1)} %copy-done, bf16[512,576]{1,0:T(8,128)(2,1)} %copy.104.other, bf16[576,768]{1,0:T(8,128)(2,1)} %fusion.chooser), custom_call_target="tpu_custom_call" | custom-call | flops 679477248 | bytes 3000000 | tf_op jit(solution)/shard_map/pallas_call | solution.py:739
  82.5 10.6 %shard_map.268 = (bf16[512,256]{1,0:T(8,128)(2,1)}, bf16[2048,256]{1,0:T(8,128)(2,1)}, bf16[2048,256]{1,0:T(8,128)(2,1)}, bf16[2048,768]{1,0:T(8,128)(2,1)}) custom-call(s32[65]{0:T(128)} %concatenate.150.meta, bf16[512,768]{1,0:T(8,128)(2,1)} %pad_maximum_fusion.2.near, bf16[512,768]{1,0:T(8,128)(2,1)} %copy-done.33, ...), custom_call_target="tpu_custom_call" | custom-call | flops 2000000000 | bytes 8000000 | tf_op jit(solution)/shard_map/pallas_call | solution.py:739
  93.2 2.2 constant_dynamic-update-slice_fusion.7
  99.4 1.8 constant_dynamic-update-slice_fusion.9
  102.7 10.9 %shard_map.269 = (f32[256,512]{1,0:T(8,128)}, f32[8,512]{1,0:T(8,128)}, bf16[4,128,192]{2,1,0:T(8,128)(2,1)}) custom-call(s32[65]{0:T(128)} %concatenate.150.meta, bf16[512,256]{1,0:T(8,128)(2,1)} %get-tuple-element.131.query_in, bf16[2048,256]{1,0:T(8,128)(2,1)} %get-tuple-element.135.key_in, bf16[2048,256]{1,0:T(8,128)(2,1)} %get-tuple-element.136.value_in), custom_call_target="tpu_custom_call" | custom-call | flops 8000000000 | bytes 4000000 | tf_op jit(solution)/shard_map/pallas_call | solution.py:739
  117.3 8.6 %collective-permute-done.16 = bf16[2,128,192]{2,1,0:T(8,128)(2,1)S(1)} collective-permute-done((bf16[2,128,192]{2,1,0:T(8,128)(2,1)S(1)}, bf16[2,128,192]{2,1,0:T(8,128)(2,1)S(1)}, u32[]{:S(2)}, u32[]{:S(2)}) %collective-permute-start.16) | collective-permute-done | bytes 98336 | tf_op jit(solution)/shard_map/ppermute | solution.py:329
  129.2 1.7 collective-permute-done.19
  134.2 2.9 shard_map.270
  139.5 13.2 %shard_map.271 = (f32[2,128,768]{2,1,0:T(8,128)}, f32[2,128,768]{2,1,0:T(8,128)}, bf16[8,384,256]{2,1,0:T(8,128)(2,1)}, bf16[8,384,128]{2,1,0:T(8,128)(2,1)}, bf...) custom-call(s32[65]{0:T(128)} %concatenate.150.meta, ...), custom_call_target="tpu_custom_call" | custom-call | flops 3600000000 | bytes 12000000 | tf_op jit(solution)/shard_map/pallas_call | solution.py:739
  156.3 4.3 %shard_map.272 = (bf16[128,768]{1,0:T(8,128)(2,1)}, f32[128,768]{1,0:T(8,128)}, bf16[128,768]{1,0:T(8,128)(2,1)}, bf16[768,768]{1,0:T(8,128)(2,1)}, f32[8,768]{1,0:T(8,128)}) custom-call(s32[65]{0:T(128)} %concatenate.150.meta, f32[2,128,768]{2,1,0:T(8,128)} %get-tuple-element.147.sums_own, f32[2,128,768]{2,1,0:T(8,128)} %copy-done.13, ...), custom_call_target="tpu_custom_call" | custom-call | flops 300000000 | bytes 5000000 | tf_op jit(solution)/shard_map/pallas_call | solution.py:739
  163.9 3.8 %collective-permute-done.26 = bf16[2,128,192]{1,2,0:T(8,128)(2,1)S(1)} collective-permute-done((bf16[2,128,192]{1,2,0:T(8,128)(2,1)S(1)}, bf16[2,128,192]{1,2,0:T(8,128)(2,1)S(1)}, u32[]{:S(2)}, u32[]{:S(2)}) %collective-permute-start.26) | collective-permute-done | bytes 98336 | tf_op jit(solution)/shard_map/ppermute | solution.py:329
  171.1 2.2 collective-permute-done.27
  175.2 15.4 %shard_map.273 = (bf16[512,256]{1,0:T(8,128)(2,1)}, f32[2048,256]{1,0:T(8,128)}, f32[2048,256]{1,0:T(8,128)}) custom-call(s32[65]{0:T(128)} %concatenate.150.meta, f32[2048,128]{1,0:T(8,128)} %bitcast.308, f32[2048,128]{1,0:T(8,128)} %bitcast.305, bf16[512,256]{1,0:T(8,128)(2,1)} %get-tuple-element.131.query_in, ...), custom_call_target="tpu_custom_call" | custom-call | flops 14000000000 | bytes 8000000 | tf_op jit(solution)/shard_map/pallas_call | solution.py:739
  190.7 1.8 maximum_select_fusion.3
  193.7 1.8 add_convert_fusion
  196.5 2.5 collective-permute-start.32
  203.6 13.8 %shard_map.274 = (bf16[1024,768]{1,0:T(8,128)(2,1)}, bf16[1024,768]{1,0:T(8,128)(2,1)}, bf16[768,576]{1,0:T(8,128)(2,1)}, f32[768,2]{1,0:T(8,128)}) custom-call(s32[65]{0:T(128)} %concatenate.150.meta, bf16[2048,768]{1,0:T(8,128)(2,1)} %get-tuple-element.162.norm, bf16[768,768]{1,0:T(8,128)(2,1)} %shard_map.267.weight, bf16[576,768]{1,0:T(8,128)(2,1)} %fusion.chooser, ...), custom_call_target="tpu_custom_call" | custom-call | flops 6000000000 | bytes 16000000 | tf_op jit(solution)/shard_map/pallas_call | solution.py:739
  221.8 1.6 collective-permute-start.38
  226.4 4.5 %collective-permute-done.39 = bf16[768,128]{1,0:T(8,128)(2,1)S(1)} collective-permute-done((bf16[768,128]{1,0:T(8,128)(2,1)S(1)}, bf16[768,128]{1,0:T(8,128)(2,1)S(1)}, u32[]{:S(2)}, u32[]{:S(2)}) %collective-permute-start.39) | collective-permute-done | bytes 196640 | tf_op jit(solution)/shard_map/ppermute | solution.py:329
  230.9 1.8 fusion.3
  234.2 1.6 collective-permute-start.41
  236.1 7.0 %collective-permute-done.41 = bf16[2,2,48,576]{3,2,0,1:T(8,128)(2,1)S(1)} collective-permute-done((bf16[2,2,48,576]{3,2,0,1:T(8,128)(2,1)S(1)}, bf16[2,2,48,576]{3,2,0,1:T(8,128)(2,1)S(1)}, u32[]{:S(2)}, u32[]{:S(2)}) %collective-permute-start.41) | collective-permute-done | bytes 221216 | tf_op jit(solution)/shard_map/ppermute | solution.py:329
  243.2 2.2 collective-permute-done.40
  245.4 4.3 %collective-permute-done.42 = bf16[384,384]{1,0:T(8,128)(2,1)S(1)} collective-permute-done((bf16[384,384]{1,0:T(8,128)(2,1)S(1)}, bf16[384,384]{1,0:T(8,128)(2,1)S(1)}, u32[]{:S(2)}, u32[]{:S(2)}) %collective-permute-start.42) | collective-permute-done | bytes 294944 | tf_op jit(solution)/shard_map/ppermute | solution.py:329
  251.7 1.8 collective-permute-start.43
  253.6 1.8 collective-permute-start.45
  255.4 7.0 %collective-permute-done.44 = bf16[192,960]{1,0:T(8,128)(2,1)S(1)} collective-permute-done((bf16[192,960]{1,0:T(8,128)(2,1)S(1)}, bf16[192,960]{1,0:T(8,128)(2,1)S(1)}, u32[]{:S(2)}, u32[]{:S(2)}) %collective-permute-start.44) | collective-permute-done | bytes 368672 | tf_op jit(solution)/shard_map/ppermute | solution.py:329
  268.5 1.8 collective-permute-start.46
  273.0 6.6 %collective-permute-done.46 = bf16[160,768]{1,0:T(8,128)(2,1)S(1)} collective-permute-done((bf16[160,768]{1,0:T(8,128)(2,1)S(1)}, bf16[160,768]{1,0:T(8,128)(2,1)S(1)}, u32[]{:S(2)}, u32[]{:S(2)}) %collective-permute-start.46) | collective-permute-done | bytes 245792 | tf_op jit(solution)/shard_map/ppermute | solution.py:329
  280.3 3.1 %collective-permute-start.49 = (f32[9,768]{1,0:T(8,128)S(1)}, f32[9,768]{1,0:T(8,128)S(1)}, u32[]{:S(2)}, u32[]{:S(2)}) collective-permute-start(f32[9,768]{1,0:T(8,128)S(1)} %convert_add_fusion.14), channel_id=1, source_target_pairs={{0,8},{1,9},{2,10},{3,11},{4,12},{5,13},{6,14},{7,15},{8,0},{9,1},... | collective-permute-start | bytes 82952 | tf_op jit(solution)/shard_map/ppermute | solution.py:329
  283.4 2.3 shard_map.275
  286.7 1.6 reshape.1167
  299.0 2.9 collective-permute-done.51
  (387 shorter events, 102.4 us)
Async XLA Ops:
  1.6 14.0 %collective-permute-start = (bf16[64,768]{1,0:T(8,128)(2,1)S(1)}, bf16[64,768]{1,0:T(8,128)(2,1)S(1)}, u32[]{:S(2)}, u32[]{:S(2)}) collective-permute-start(bf16[64,768]{1,0:T(8,128)(2,1)S(1)} %get-tuple-element.263), channel_id=1, source_target_pairs={{0,8},{1,9},{2,10},{3,11},{4,12},{5,13},{6,14},{7,15},{8,0},{9,1},... | collective-permute-start | bytes 294920 | tf_op jit(solution)/shard_map/ppermute | solution.py:329
  18.3 8.0 %collective-permute-start.1 = (bf16[128,768]{1,0:T(8,128)(2,1)S(1)}, bf16[128,768]{1,0:T(8,128)(2,1)S(1)}, u32[]{:S(2)}, u32[]{:S(2)}) collective-permute-start(bf16[128,768]{1,0:T(8,128)(2,1)S(1)} %pad_maximum_fusion.22.own_rows.source), channel_id=1, source_target_pairs={{0,4},{1,5},{2,6},{3,7},{4,0},{5,1},{6,2},{7,3},{8,12},{9,13},{10,... | collective-permute-start | bytes 589832 | tf_op jit(solution)/shard_map/ppermute | solution.py:329
  20.8 22.8 %collective-permute-start.4 = (bf16[208,576]{1,0:T(8,128)(2,1)S(1)}, bf16[208,576]{1,0:T(8,128)(2,1)S(1)}, u32[]{:S(2)}, u32[]{:S(2)}) collective-permute-start(bf16[208,576]{1,0:T(8,128)(2,1)S(1)} %pad_maximum_fusion.17), channel_id=1, source_target_pairs={{0,8},{1,9},{2,10},{3,11},{4,12},{5,13},{6,14},{7,15},{8,0},{9,1},... | collective-permute-start | bytes 718856 | tf_op jit(solution)/shard_map/ppermute | solution.py:329
  26.4 9.2 %collective-permute-start.3 = (bf16[256,768]{1,0:T(8,128)(2,1)S(1)}, bf16[256,768]{1,0:T(8,128)(2,1)S(1)}, u32[]{:S(2)}, u32[]{:S(2)}) collective-permute-start(bf16[256,768]{1,0:T(8,128)(2,1)S(1)} %pad_maximum_fusion.7), channel_id=1, source_target_pairs={{0,2},{1,17},{2,0},{3,19},{4,6},{5,21},{6,4},{7,23},{8,10},{9,25},... | collective-permute-start | bytes 1179656 | tf_op jit(solution)/shard_map/ppermute | solution.py:329
  30.5 19.7 %collective-permute-start.7 = (bf16[432,384]{1,0:T(8,128)(2,1)S(1)}, bf16[432,384]{1,0:T(8,128)(2,1)S(1)}, u32[]{:S(2)}, u32[]{:S(2)}) collective-permute-start(bf16[432,384]{1,0:T(8,128)(2,1)S(1)} %pad_maximum_fusion.9), channel_id=1, source_target_pairs={{0,8},{1,9},{2,10},{3,11},{4,12},{5,13},{6,14},{7,15},{8,0},{9,1},... | collective-permute-start | bytes 995336 | tf_op jit(solution)/shard_map/ppermute | solution.py:329
  43.8 9.2 %collective-permute-start.6 = (bf16[224,576]{1,0:T(8,128)(2,1)S(1)}, bf16[224,576]{1,0:T(8,128)(2,1)S(1)}, u32[]{:S(2)}, u32[]{:S(2)}) collective-permute-start(bf16[224,576]{1,0:T(8,128)(2,1)S(1)} %pad_maximum_fusion.16), channel_id=1, source_target_pairs={{0,2},{1,3},{2,0},{3,1},{4,6},{5,7},{6,4},{7,5},{8,10},{9,11},{10,... | collective-permute-start | bytes 774152 | tf_op jit(solution)/shard_map/ppermute | solution.py:329
  45.4 20.2 %collective-permute-start.5 = (bf16[512,768]{1,0:T(8,128)(2,1)}, bf16[512,768]{1,0:T(8,128)(2,1)S(1)}, u32[]{:S(2)}, u32[]{:S(2)}) collective-permute-start(bf16[512,768]{1,0:T(8,128)(2,1)} %pad_maximum_fusion.2.near), channel_id=1, source_target_pairs={{0,16},{1,3},{2,18},{3,1},{4,20},{5,7},{6,22},{7,5},{8,24},{9,11},... | collective-permute-start | bytes 2359304 | tf_op jit(solution)/shard_map/ppermute | solution.py:329
  53.2 9.0 %collective-permute-start.9 = (bf16[1,2,432,256]{3,2,1,0:T(8,128)(2,1)S(1)}, bf16[1,2,432,256]{3,2,1,0:T(8,128)(2,1)S(1)}, u32[]{:S(2)}, u32[]{:S(2)}) collective-permute-start(bf16[1,2,432,256]{3,2,1,0:T(8,128)(2,1)S(1)} %slice.434), channel_id=1, source_target_pairs={{0,2},{1,17},{2,0},{3,19},{4,6},{5,21},{6,4},{7,23},{8,10},{9,25},... | collective-permute-start | bytes 1327112 | tf_op jit(solution)/shard_map/ppermute | solution.py:329
  54.8 7.4 %collective-permute-start.10 = (bf16[1,2,432,128]{3,2,1,0:T(8,128)(2,1)S(1)}, bf16[1,2,432,128]{3,2,1,0:T(8,128)(2,1)S(1)}, u32[]{:S(2)}, u32[]{:S(2)}) collective-permute-start(bf16[1,2,432,128]{3,2,1,0:T(8,128)(2,1)S(1)} %slice.435), channel_id=1, source_target_pairs={{0,4},{1,5},{2,6},{3,7},{4,0},{5,1},{6,2},{7,3},{8,12},{9,13},{10,... | collective-permute-start | bytes 663560 | tf_op jit(solution)/shard_map/ppermute | solution.py:329
  54.9 10.8 %collective-permute-start.8 = (bf16[256,576]{1,0:T(8,128)(2,1)S(1)}, bf16[256,576]{1,0:T(8,128)(2,1)S(1)}, u32[]{:S(2)}, u32[]{:S(2)}) collective-permute-start(bf16[256,576]{1,0:T(8,128)(2,1)S(1)} %pad_maximum_fusion.10), channel_id=1, source_target_pairs={{0,4},{1,5},{2,6},{3,7},{4,0},{5,1},{6,2},{7,3},{8,12},{9,13},{10,... | collective-permute-start | bytes 884744 | tf_op jit(solution)/shard_map/ppermute | solution.py:329
  66.8 5.0 %collective-permute-start.13 = (bf16[512,576]{0,1:T(8,128)(2,1)S(1)}, bf16[512,576]{0,1:T(8,128)(2,1)S(1)}, u32[]{:S(2)}, u32[]{:S(2)}) collective-permute-start(bf16[512,576]{0,1:T(8,128)(2,1)S(1)} %copy.103), channel_id=1, source_target_pairs={{0,1},{1,0},{2,3},{3,2},{4,5},{5,4},{6,7},{7,6},{8,9},{9,8},{10,11... | collective-permute-start | bytes 1769480 | tf_op jit(solution)/shard_map/ppermute | solution.py:329
  66.9 15.6 %collective-permute-start.11 = (bf16[512,768]{1,0:T(8,128)(2,1)}, bf16[512,768]{1,0:T(8,128)(2,1)}, u32[]{:S(2)}, u32[]{:S(2)}) collective-permute-start(bf16[512,768]{1,0:T(8,128)(2,1)} %pad_maximum_fusion.2.near), channel_id=1, source_target_pairs={{0,1},{1,0},{2,3},{3,2},{4,5},{5,4},{6,7},{7,6},{8,9},{9,8},{10,11... | collective-permute-start | bytes 2359304 | tf_op jit(solution)/shard_map/ppermute | solution.py:329
  69.2 13.3 %collective-permute-start.12 = (bf16[512,768]{1,0:T(8,128)(2,1)}, bf16[512,768]{1,0:T(8,128)(2,1)}, u32[]{:S(2)}, u32[]{:S(2)}) collective-permute-start(bf16[512,768]{1,0:T(8,128)(2,1)} %copy-done.33), channel_id=1, source_target_pairs={{0,1},{1,0},{2,3},{3,2},{4,5},{5,4},{6,7},{7,6},{8,9},{9,8},{10,11... | collective-permute-start | bytes 2359304 | tf_op jit(solution)/shard_map/ppermute | solution.py:329
  70.0 23.2 %collective-permute-start.14 = (bf16[2,2,432,256]{3,2,1,0:T(8,128)(2,1)S(1)}, bf16[2,2,432,256]{3,2,1,0:T(8,128)(2,1)}, u32[]{:S(2)}, u32[]{:S(2)}) collective-permute-start(bf16[2,2,432,256]{3,2,1,0:T(8,128)(2,1)S(1)} %pad_maximum_fusion), channel_id=1, source_target_pairs={{0,4},{1,3},{2,6},{3,1},{4,0},{5,7},{6,2},{7,5},{8,12},{9,11},{10,... | collective-permute-start | bytes 2654216 | tf_op jit(solution)/shard_map/ppermute | solution.py:329
  70.3 22.9 %collective-permute-start.15 = (bf16[2,2,432,128]{3,2,1,0:T(8,128)(2,1)S(1)}, bf16[2,2,432,128]{3,2,1,0:T(8,128)(2,1)}, u32[]{:S(2)}, u32[]{:S(2)}) collective-permute-start(bf16[2,2,432,128]{3,2,1,0:T(8,128)(2,1)S(1)} %pad_maximum_fusion.5), channel_id=1, source_target_pairs={{0,16},{1,17},{2,18},{3,19},{4,20},{5,21},{6,22},{7,23},{8,24},{9,... | collective-permute-start | bytes 1327112 | tf_op jit(solution)/shard_map/ppermute | solution.py:329
  95.4 30.5 %collective-permute-start.17 = (bf16[4,2,432,256]{3,2,1,0:T(8,128)(2,1)}, bf16[4,2,432,256]{3,2,1,0:T(8,128)(2,1)}, u32[]{:S(2)}, u32[]{:S(2)}) collective-permute-start(bf16[4,2,432,256]{3,2,1,0:T(8,128)(2,1)} %constant_dynamic-update-slice_fusion.7), channel_id=1, source_target_pairs={{0,16},{1,5},{2,18},{3,7},{4,20},{5,1},{6,22},{7,3},{8,24},{9,13},... | collective-permute-start | bytes 5308424 | tf_op jit(solution)/shard_map/ppermute | solution.py:329
  97.6 31.0 %collective-permute-start.23 = (bf16[64,768]{1,0:T(8,128)(2,1)}, bf16[64,768]{1,0:T(8,128)(2,1)S(1)}, u32[]{:S(2)}, u32[]{:S(2)}) collective-permute-start(bf16[64,768]{1,0:T(8,128)(2,1)} %get-tuple-element.261), channel_id=1, source_target_pairs={{0,8},{1,9},{2,10},{3,11},{4,12},{5,13},{6,14},{7,15},{8,0},{9,1},... | collective-permute-start | bytes 294920 | tf_op jit(solution)/shard_map/ppermute | solution.py:329
  101.2 24.7 %collective-permute-start.18 = (bf16[4,2,432,128]{3,2,1,0:T(8,128)(2,1)}, bf16[4,2,432,128]{3,2,1,0:T(8,128)(2,1)}, u32[]{:S(2)}, u32[]{:S(2)}) collective-permute-start(bf16[4,2,432,128]{3,2,1,0:T(8,128)(2,1)} %constant_dynamic-update-slice_fusion.9), channel_id=1, source_target_pairs={{0,2},{1,3},{2,0},{3,1},{4,6},{5,7},{6,4},{7,5},{8,10},{9,11},{10,... | collective-permute-start | bytes 2654216 | tf_op jit(solution)/shard_map/ppermute | solution.py:329
  114.6 11.3 %collective-permute-start.16 = (bf16[2,128,192]{2,1,0:T(8,128)(2,1)S(1)}, bf16[2,128,192]{2,1,0:T(8,128)(2,1)S(1)}, u32[]{:S(2)}, u32[]{:S(2)}) collective-permute-start(bf16[2,128,192]{2,1,0:T(8,128)(2,1)S(1)} %get-tuple-element.253), channel_id=1, source_target_pairs={{0,2},{1,3},{2,0},{3,1},{4,6},{5,7},{6,4},{7,5},{8,10},{9,11},{10,... | collective-permute-start | bytes 294920 | tf_op jit(solution)/shard_map/ppermute | solution.py:329
  117.2 15.6 %collective-permute-start.20 = (bf16[8,48,384]{2,1,0:T(8,128)(2,1)S(1)}, bf16[8,48,384]{2,1,0:T(8,128)(2,1)S(1)}, u32[]{:S(2)}, u32[]{:S(2)}) collective-permute-start(bf16[8,48,384]{2,1,0:T(8,128)(2,1)S(1)} %pad_maximum_fusion.12), channel_id=1, source_target_pairs={{0,1},{1,0},{2,3},{3,2},{4,5},{5,4},{6,7},{7,6},{8,9},{9,8},{10,11... | collective-permute-start | bytes 884744 | tf_op jit(solution)/shard_map/ppermute | solution.py:329
  126.0 5.0 %collective-permute-start.19 = (bf16[2,128,192]{2,1,0:T(8,128)(2,1)S(1)}, bf16[2,128,192]{2,1,0:T(8,128)(2,1)S(1)}, u32[]{:S(2)}, u32[]{:S(2)}) collective-permute-start(bf16[2,128,192]{2,1,0:T(8,128)(2,1)S(1)} %get-tuple-element.251), channel_id=1, source_target_pairs={{0,4},{1,5},{2,6},{3,7},{4,0},{5,1},{6,2},{7,3},{8,12},{9,13},{10,... | collective-permute-start | bytes 294920 | tf_op jit(solution)/shard_map/ppermute | solution.py:329
  128.7 10.2 %collective-permute-start.24 = (bf16[128,768]{1,0:T(8,128)(2,1)S(1)}, bf16[128,768]{1,0:T(8,128)(2,1)}, u32[]{:S(2)}, u32[]{:S(2)}) collective-permute-start(bf16[128,768]{1,0:T(8,128)(2,1)S(1)} %multiply_convert_fusion.grad_own.grad_branch), channel_id=1, source_target_pairs={{0,1},{1,0},{2,3},{3,2},{4,5},{5,4},{6,7},{7,6},{8,9},{9,8},{10,11... | collective-permute-start | bytes 589832 | tf_op jit(solution)/shard_map/ppermute | solution.py:329
  162.5 5.1 %collective-permute-start.26 = (bf16[2,128,192]{1,2,0:T(8,128)(2,1)S(1)}, bf16[2,128,192]{1,2,0:T(8,128)(2,1)S(1)}, u32[]{:S(2)}, u32[]{:S(2)}) collective-permute-start(bf16[2,128,192]{1,2,0:T(8,128)(2,1)S(1)} %get-tuple-element.259), channel_id=1, source_target_pairs={{0,2},{1,3},{2,0},{3,1},{4,6},{5,7},{6,4},{7,5},{8,10},{9,11},{10,... | collective-permute-start | bytes 294920 | tf_op jit(solution)/shard_map/ppermute | solution.py:329
  167.7 5.7 %collective-permute-start.27 = (bf16[2,128,192]{1,2,0:T(8,128)(2,1)S(1)}, bf16[2,128,192]{1,2,0:T(8,128)(2,1)S(1)}, u32[]{:S(2)}, u32[]{:S(2)}) collective-permute-start(bf16[2,128,192]{1,2,0:T(8,128)(2,1)S(1)} %get-tuple-element.257), channel_id=1, source_target_pairs={{0,4},{1,5},{2,6},{3,7},{4,0},{5,1},{6,2},{7,3},{8,12},{9,13},{10,... | collective-permute-start | bytes 294920 | tf_op jit(solution)/shard_map/ppermute | solution.py:329
  169.3 24.3 %collective-permute-start.28 = (bf16[8,384,256]{2,1,0:T(8,128)(2,1)}, bf16[8,384,256]{2,1,0:T(8,128)(2,1)}, u32[]{:S(2)}, u32[]{:S(2)}) collective-permute-start(bf16[8,384,256]{2,1,0:T(8,128)(2,1)} %get-tuple-element.157), channel_id=1, source_target_pairs={{0,16},{1,5},{2,18},{3,7},{4,20},{5,1},{6,22},{7,3},{8,24},{9,13},... | collective-permute-start | bytes 4718600 | tf_op jit(solution)/shard_map/ppermute | solution.py:329
  170.6 23.0 %collective-permute-start.29 = (bf16[8,384,128]{2,1,0:T(8,128)(2,1)}, bf16[8,384,128]{2,1,0:T(8,128)(2,1)}, u32[]{:S(2)}, u32[]{:S(2)}) collective-permute-start(bf16[8,384,128]{2,1,0:T(8,128)(2,1)} %get-tuple-element.158), channel_id=1, source_target_pairs={{0,2},{1,3},{2,0},{3,1},{4,6},{5,7},{6,4},{7,5},{8,10},{9,11},{10,... | collective-permute-start | bytes 2359304 | tf_op jit(solution)/shard_map/ppermute | solution.py:329
  174.3 18.2 %collective-permute-start.30 = (bf16[8,48,768]{2,1,0:T(8,128)(2,1)S(1)}, bf16[8,48,768]{2,1,0:T(8,128)(2,1)}, u32[]{:S(2)}, u32[]{:S(2)}) collective-permute-start(bf16[8,48,768]{2,1,0:T(8,128)(2,1)S(1)} %dynamic-slice_bitcast_fusion), channel_id=1, source_target_pairs={{0,1},{1,0},{2,3},{3,2},{4,5},{5,4},{6,7},{7,6},{8,9},{9,8},{10,11... | collective-permute-start | bytes 1769480 | tf_op jit(solution)/shard_map/ppermute | solution.py:329
  174.4 16.3 %collective-permute-start.31 = (bf16[64,768]{1,0:T(8,128)(2,1)S(1)}, bf16[64,768]{1,0:T(8,128)(2,1)}, u32[]{:S(2)}, u32[]{:S(2)}) collective-permute-start(bf16[64,768]{1,0:T(8,128)(2,1)S(1)} %get-tuple-element.255), channel_id=1, source_target_pairs={{0,8},{1,9},{2,10},{3,11},{4,12},{5,13},{6,14},{7,15},{8,0},{9,1},... | collective-permute-start | bytes 294920 | tf_op jit(solution)/shard_map/ppermute | solution.py:329
  196.5 21.0 %collective-permute-start.32 = (bf16[2,768,256]{2,1,0:T(8,128)(2,1)}, bf16[2,768,256]{2,1,0:T(8,128)(2,1)}, u32[]{:S(2)}, u32[]{:S(2)}) collective-permute-start(bf16[2,768,256]{2,1,0:T(8,128)(2,1)} %bitcast.89), channel_id=1, source_target_pairs={{0,4},{1,3},{2,6},{3,1},{4,0},{5,7},{6,2},{7,5},{8,12},{9,11},{10,... | collective-permute-start | bytes 2359304 | tf_op jit(solution)/shard_map/ppermute | solution.py:329
  201.1 16.4 %collective-permute-start.33 = (bf16[2,768,128]{2,1,0:T(8,128)(2,1)}, bf16[2,768,128]{2,1,0:T(8,128)(2,1)}, u32[]{:S(2)}, u32[]{:S(2)}) collective-permute-start(bf16[2,768,128]{2,1,0:T(8,128)(2,1)} %bitcast.90), channel_id=1, source_target_pairs={{0,16},{1,17},{2,18},{3,19},{4,20},{5,21},{6,22},{7,23},{8,24},{9,... | collective-permute-start | bytes 1179656 | tf_op jit(solution)/shard_map/ppermute | solution.py:329
  203.1 14.4 %collective-permute-start.34 = (bf16[2,2,48,768]{3,2,1,0:T(8,128)(2,1)}, bf16[2,2,48,768]{3,2,1,0:T(8,128)(2,1)}, u32[]{:S(2)}, u32[]{:S(2)}) collective-permute-start(bf16[2,2,48,768]{3,2,1,0:T(8,128)(2,1)} %dynamic-slice_bitcast_fusion.2), channel_id=1, source_target_pairs={{0,2},{1,3},{2,0},{3,1},{4,6},{5,7},{6,4},{7,5},{8,10},{9,11},{10,... | collective-permute-start | bytes 884744 | tf_op jit(solution)/shard_map/ppermute | solution.py:329
  217.5 13.4 %collective-permute-start.35 = (bf16[1024,768]{1,0:T(8,128)(2,1)}, bf16[1024,768]{1,0:T(8,128)(2,1)}, u32[]{:S(2)}, u32[]{:S(2)}) collective-permute-start(bf16[1024,768]{1,0:T(8,128)(2,1)} %get-tuple-element.176), channel_id=1, source_target_pairs={{0,1},{1,0},{2,3},{3,2},{4,5},{5,4},{6,7},{7,6},{8,9},{9,8},{10,11... | collective-permute-start | bytes 4718600 | tf_op jit(solution)/shard_map/ppermute | solution.py:329
  218.7 7.4 %collective-permute-start.36 = (f32[7,768]{1,0:T(8,128)S(1)}, f32[7,768]{1,0:T(8,128)S(1)}, u32[]{:S(2)}, u32[]{:S(2)}) collective-permute-start(f32[7,768]{1,0:T(8,128)S(1)} %pad_maximum_fusion.28), channel_id=1, source_target_pairs={{0,1},{1,0},{2,3},{3,2},{4,5},{5,4},{6,7},{7,6},{8,9},{9,8},{10,11... | collective-permute-start | bytes 64520 | tf_op jit(solution)/shard_map/ppermute | solution.py:329
  220.4 5.9 %collective-permute-start.37 = (bf16[8,48,576]{2,1,0:T(8,128)(2,1)S(1)}, bf16[8,48,576]{2,1,0:T(8,128)(2,1)S(1)}, u32[]{:S(2)}, u32[]{:S(2)}) collective-permute-start(bf16[8,48,576]{2,1,0:T(8,128)(2,1)S(1)} %dynamic-slice_bitcast_fusion.1), channel_id=1, source_target_pairs={{0,1},{1,0},{2,3},{3,2},{4,5},{5,4},{6,7},{7,6},{8,9},{9,8},{10,11... | collective-permute-start | bytes 1327112 | tf_op jit(solution)/shard_map/ppermute | solution.py:329
  221.8 9.1 %collective-permute-start.38 = (bf16[768,256]{1,0:T(8,128)(2,1)S(1)}, bf16[768,256]{1,0:T(8,128)(2,1)S(1)}, u32[]{:S(2)}, u32[]{:S(2)}) collective-permute-start(bf16[768,256]{1,0:T(8,128)(2,1)S(1)} %slice_bitcast_fusion.1), channel_id=1, source_target_pairs={{0,2},{1,17},{2,0},{3,19},{4,6},{5,21},{6,4},{7,23},{8,10},{9,25},... | collective-permute-start | bytes 1179656 | tf_op jit(solution)/shard_map/ppermute | solution.py:329
  224.6 6.3 %collective-permute-start.39 = (bf16[768,128]{1,0:T(8,128)(2,1)S(1)}, bf16[768,128]{1,0:T(8,128)(2,1)S(1)}, u32[]{:S(2)}, u32[]{:S(2)}) collective-permute-start(bf16[768,128]{1,0:T(8,128)(2,1)S(1)} %slice_bitcast_fusion.4), channel_id=1, source_target_pairs={{0,4},{1,5},{2,6},{3,7},{4,0},{5,1},{6,2},{7,3},{8,12},{9,13},{10,... | collective-permute-start | bytes 589832 | tf_op jit(solution)/shard_map/ppermute | solution.py:329
  232.8 12.6 %collective-permute-start.40 = (bf16[544,768]{1,0:T(8,128)(2,1)S(1)}, bf16[544,768]{1,0:T(8,128)(2,1)S(1)}, u32[]{:S(2)}, u32[]{:S(2)}) collective-permute-start(bf16[544,768]{1,0:T(8,128)(2,1)S(1)} %pad_maximum_fusion.1), channel_id=1, source_target_pairs={{0,16},{1,3},{2,18},{3,1},{4,20},{5,7},{6,22},{7,5},{8,24},{9,11},... | collective-permute-start | bytes 2506760 | tf_op jit(solution)/shard_map/ppermute | solution.py:329
  234.2 8.9 %collective-permute-start.41 = (bf16[2,2,48,576]{3,2,0,1:T(8,128)(2,1)S(1)}, bf16[2,2,48,576]{3,2,0,1:T(8,128)(2,1)S(1)}, u32[]{:S(2)}, u32[]{:S(2)}) collective-permute-start(bf16[2,2,48,576]{3,2,0,1:T(8,128)(2,1)S(1)} %bitcast.342), channel_id=1, source_target_pairs={{0,2},{1,3},{2,0},{3,1},{4,6},{5,7},{6,4},{7,5},{8,10},{9,11},{10,... | collective-permute-start | bytes 663560 | tf_op jit(solution)/shard_map/ppermute | solution.py:329
  236.0 13.7 %collective-permute-start.42 = (bf16[384,384]{1,0:T(8,128)(2,1)S(1)}, bf16[384,384]{1,0:T(8,128)(2,1)S(1)}, u32[]{:S(2)}, u32[]{:S(2)}) collective-permute-start(bf16[384,384]{1,0:T(8,128)(2,1)S(1)} %fusion.13), channel_id=1, source_target_pairs={{0,8},{1,9},{2,10},{3,11},{4,12},{5,13},{6,14},{7,15},{8,0},{9,1},... | collective-permute-start | bytes 884744 | tf_op jit(solution)/shard_map/ppermute | solution.py:329
  251.4 11.0 %collective-permute-start.44 = (bf16[192,960]{1,0:T(8,128)(2,1)S(1)}, bf16[192,960]{1,0:T(8,128)(2,1)S(1)}, u32[]{:S(2)}, u32[]{:S(2)}) collective-permute-start(bf16[192,960]{1,0:T(8,128)(2,1)S(1)} %pad_maximum_fusion.8), channel_id=1, source_target_pairs={{0,4},{1,5},{2,6},{3,7},{4,0},{5,1},{6,2},{7,3},{8,12},{9,13},{10,... | collective-permute-start | bytes 1105928 | tf_op jit(solution)/shard_map/ppermute | solution.py:329
  251.7 13.0 %collective-permute-start.43 = (bf16[288,768]{1,0:T(8,128)(2,1)S(1)}, bf16[288,768]{1,0:T(8,128)(2,1)}, u32[]{:S(2)}, u32[]{:S(2)}) collective-permute-start(bf16[288,768]{1,0:T(8,128)(2,1)S(1)} %pad_maximum_fusion.6), channel_id=1, source_target_pairs={{0,2},{1,17},{2,0},{3,19},{4,6},{5,21},{6,4},{7,23},{8,10},{9,25},... | collective-permute-start | bytes 1327112 | tf_op jit(solution)/shard_map/ppermute | solution.py:329
  253.6 13.0 %collective-permute-start.45 = (bf16[384,384]{1,0:T(8,128)(2,1)S(1)}, bf16[384,384]{1,0:T(8,128)(2,1)}, u32[]{:S(2)}, u32[]{:S(2)}) collective-permute-start(bf16[384,384]{1,0:T(8,128)(2,1)S(1)} %fusion.8), channel_id=1, source_target_pairs={{0,16},{1,17},{2,18},{3,19},{4,20},{5,21},{6,22},{7,23},{8,24},{9,... | collective-permute-start | bytes 884744 | tf_op jit(solution)/shard_map/ppermute | solution.py:329
  266.9 21.4 %collective-permute-start.48 = (bf16[192,768]{1,0:T(8,128)(2,1)S(1)}, bf16[192,768]{1,0:T(8,128)(2,1)S(1)}, u32[]{:S(2)}, u32[]{:S(2)}) collective-permute-start(bf16[192,768]{1,0:T(8,128)(2,1)S(1)} %pad_maximum_fusion.14), channel_id=1, source_target_pairs={{0,8},{1,9},{2,10},{3,11},{4,12},{5,13},{6,14},{7,15},{8,0},{9,1},... | collective-permute-start | bytes 884744 | tf_op jit(solution)/shard_map/ppermute | solution.py:329
  268.5 11.1 %collective-permute-start.46 = (bf16[160,768]{1,0:T(8,128)(2,1)S(1)}, bf16[160,768]{1,0:T(8,128)(2,1)S(1)}, u32[]{:S(2)}, u32[]{:S(2)}) collective-permute-start(bf16[160,768]{1,0:T(8,128)(2,1)S(1)} %pad_maximum_fusion.21), channel_id=1, source_target_pairs={{0,4},{1,5},{2,6},{3,7},{4,0},{5,1},{6,2},{7,3},{8,12},{9,13},{10,... | collective-permute-start | bytes 737288 | tf_op jit(solution)/shard_map/ppermute | solution.py:329
  271.3 9.0 %collective-permute-start.47 = (bf16[192,384]{1,0:T(8,128)(2,1)S(1)}, bf16[192,384]{1,0:T(8,128)(2,1)S(1)}, u32[]{:S(2)}, u32[]{:S(2)}) collective-permute-start(bf16[192,384]{1,0:T(8,128)(2,1)S(1)} %get-tuple-element.237), channel_id=1, source_target_pairs={{0,1},{1,0},{2,3},{3,2},{4,5},{5,4},{6,7},{7,6},{8,9},{9,8},{10,11... | collective-permute-start | bytes 442376 | tf_op jit(solution)/shard_map/ppermute | solution.py:329
  280.3 10.0 %collective-permute-start.49 = (f32[9,768]{1,0:T(8,128)S(1)}, f32[9,768]{1,0:T(8,128)S(1)}, u32[]{:S(2)}, u32[]{:S(2)}) collective-permute-start(f32[9,768]{1,0:T(8,128)S(1)} %convert_add_fusion.14), channel_id=1, source_target_pairs={{0,8},{1,9},{2,10},{3,11},{4,12},{5,13},{6,14},{7,15},{8,0},{9,1},... | collective-permute-start | bytes 82952 | tf_op jit(solution)/shard_map/ppermute | solution.py:329
  285.7 6.1 %collective-permute-start.50 = (bf16[64,768]{1,0:T(8,128)(2,1)}, bf16[64,768]{1,0:T(8,128)(2,1)S(1)}, u32[]{:S(2)}, u32[]{:S(2)}) collective-permute-start(bf16[64,768]{1,0:T(8,128)(2,1)} %get-tuple-element.203), channel_id=1, source_target_pairs={{0,8},{1,9},{2,10},{3,11},{4,12},{5,13},{6,14},{7,15},{8,0},{9,1},... | collective-permute-start | bytes 294920 | tf_op jit(solution)/shard_map/ppermute | solution.py:329
  293.6 8.3 %collective-permute-start.51 = (bf16[48,3072]{1,0:T(8,128)(2,1)S(1)}, bf16[48,3072]{1,0:T(8,128)(2,1)S(1)}, u32[]{:S(2)}, u32[]{:S(2)}) collective-permute-start(bf16[48,3072]{1,0:T(8,128)(2,1)S(1)} %pad_maximum_fusion.15), channel_id=1, source_target_pairs={{0,16},{1,17},{2,18},{3,19},{4,20},{5,21},{6,22},{7,23},{8,24},{9,... | collective-permute-start | bytes 884744 | tf_op jit(solution)/shard_map/ppermute | solution.py:329
  (39 other events, 237.3 us)
where the time goes:
time: 305 us; the launch traced here: 303 us
  Pallas kernels  81.5 us (27%)
  waiting for transfers between devices  78.8 us (26%)
  local copies, waits for them, and re-layouts  60.3 us (20%)
  starting transfers between devices  50 us (16%)
  other arithmetic  30.7 us (10%)
    pallas_call x11, Pallas kernels, call(): pl.pallas_call(body, grid=() if grid is None else grid, out_shape=[jax.Sh...  81.5 us
    ppermute x52, waiting for transfers between devices, swap_bits(): lax.ppermute(values, AXES, [(i, i ^ (odd if i & 1 else even)) for i in ra...  78.8 us
    ppermute x52, starting transfers between devices, swap_bits(): lax.ppermute(values, AXES, [(i, i ^ (odd if i & 1 else even)) for i in ra...  50 us
    convert_element_type x17, other arithmetic, plus(): return (left.astype(f32) + right.astype(f32)).astype(bf16)  10.4 us
    unnamed x81, local copies, waits for them, and re-layouts  8.9 us
  transfers between devices with their start and end apart: 52, of which 19 were waited for; matrix products, arithmetic and copies ran while one was open for 23% of the time, Pallas kernels for 20%

commit v1 on v0

--- a/solution.py
+++ b/solution.py
@@ -410,8 +410,13 @@
     for target, which in ((own, core), (sent, 1 - core)):
         wanted = jnp.where(lane < 192, lane, lane + 192) + which * 192
         chosen = (source == wanted).astype(jnp.float32).astype(jnp.bfloat16)
-        for i in range(4):
-            target[i * 48 : (i + 1) * 48, :] = dot_nn(w_in[:, i * 768 : (i + 1) * 768], chosen).astype(jnp.bfloat16)
+
+        def body(i, carry, target=target, chosen=chosen):
+            columns = w_in[:, pl.ds(pl.multiple_of(i * 768, 128), 768)]
+            target[pl.ds(pl.multiple_of(i * 48, 16), 48), :] = dot_nn(columns, chosen).astype(jnp.bfloat16)
+            return carry
+
+        lax.fori_loop(0, 4, body, 0)
         target[192:240, :] = w_out[:, pl.ds(pl.multiple_of(which * 384, 128), 384)]
     rows = pl.ds(pl.multiple_of(side * 96, 32), 96)
     own[240:336, :] = w_down[rows, 0:384]
@@ -434,46 +439,46 @@
 
 
 def order_weight_kernel(meta, own, other, chooser, out, gathered):
-    for slot in range(16):
-        start = pl.multiple_of(meta[48 + slot] * 48, 16)
-        first = (slot % 8) * 48
-        gathered[pl.ds(start, 48), :] = (own if slot < 8 else other)[first : first + 48, :]
+    for base, source in ((48, own), (56, other)):
+
+        def body(slot, carry, base=base, source=source):
+            start = pl.multiple_of(meta[base + slot] * 48, 16)
+            gathered[pl.ds(start, 48), :] = source[pl.ds(pl.multiple_of(slot * 48, 16), 48), :]
+            return carry
+
+        lax.fori_loop(0, 8, body, 0)
     out[...] = dot_nn(gathered[...], chooser[...]).astype(jnp.bfloat16)
 
 
 def project_kernel(
-    meta, near, far, other_near, other_far, weight, vectors, cosine, sine, query_out, key_out, value_out, norm_out, all_queries
+    meta, near, far, other_near, other_far, weight, vectors, cosine, sine, query_out, key_out, value_out, norm_out, all_queries, chunk
 ):
     step = pl.program_id(0)
     rows = near.shape[0]
 
-    def project(source):
-        norm = row_norm(source[...].astype(jnp.float32))
-        norm_out[...] = norm.astype(jnp.bfloat16)
-        attn_in = (norm * vectors[8:9, :] + vectors[2:3, :]).astype(jnp.bfloat16)
-        packed = dot_nn(attn_in, weight[:, 256:768])
-        first, second = packed[:, 0:128], packed[:, 128:256]
-        turn_c, turn_s = cosine[...], sine[...]
-        key_out[:, 0:128] = (first * turn_c - second * turn_s).astype(jnp.bfloat16)
-        key_out[:, 128:256] = (second * turn_c + first * turn_s).astype(jnp.bfloat16)
-        value_out[...] = packed[:, 256:512].astype(jnp.bfloat16)
-        return attn_in
-
-    def project_queries(attn_in):
+    for number, source in enumerate((near, far, other_near, other_far)):
+
+        @pl.when(step // 2 == number)
+        def _(source=source):
+            chunk[...] = source[...]
+
+    norm = row_norm(chunk[...].astype(jnp.float32))
+    norm_out[...] = norm.astype(jnp.bfloat16)
+    attn_in = (norm * vectors[8:9, :] + vectors[2:3, :]).astype(jnp.bfloat16)
+    turn_c, turn_s = cosine[...], sine[...]
+    packed = dot_nn(attn_in, weight[:, 256:768])
+    first, second = packed[:, 0:128], packed[:, 128:256]
+    key_out[:, 0:128] = (first * turn_c - second * turn_s).astype(jnp.bfloat16)
+    key_out[:, 128:256] = (second * turn_c + first * turn_s).astype(jnp.bfloat16)
+    value_out[...] = packed[:, 256:512].astype(jnp.bfloat16)
+
+    @pl.when(step < 4)
+    def _():
         packed = dot_nn(attn_in, weight[:, 0:256]) * (HDIM ** (-0.5))
         first, second = packed[:, 0:128], packed[:, 128:256]
-        turn_c, turn_s = cosine[...], sine[...]
         here = pl.ds(pl.multiple_of(step * rows, 256), rows)
         all_queries[here, 0:128] = (first * turn_c - second * turn_s).astype(jnp.bfloat16)
         all_queries[here, 128:256] = (second * turn_c + first * turn_s).astype(jnp.bfloat16)
-
-    for number, source in enumerate((near, far, other_near, other_far)):
-
-        @pl.when(step // 2 == number)
-        def _(number=number, source=source):
-            attn_in = project(source)
-            if number < 2:
-                project_queries(attn_in)
 
     @pl.when(step == 3)
     def _():
@@ -528,23 +533,25 @@
     lane = lax.broadcasted_iota(jnp.int32, (1, 256), 1)
 
     def body(number, carry):
-        head = number % 3
-        here = pl.ds(pl.multiple_of(number // 3 * 256, 256), 256)
-        query = query_in[here, :]
-        query = jnp.where(head_select(256, head), query, jnp.zeros_like(query))
-        head_grad = grad_out[here, :]
-        head_grad = jnp.where(lane // 64 == head, head_grad, jnp.zeros_like(head_grad))
-        probs = jnp.exp(contract_cols(keys, query) - log_in[pl.ds(head, 1), here])
-        delta = jnp.sum(product[pl.ds(pl.multiple_of(head * 64, 64), 64), here], 0, keepdims=True)
-        grad_scores = (probs * (contract_cols(values, head_grad) - delta)).astype(jnp.bfloat16)
-        value_sum[...] += dot_nn(probs.astype(jnp.bfloat16), head_grad)
-        key_sum[...] += dot_nn(grad_scores, query)
-        part = dot_nn(key_turned, grad_scores).T * (HDIM ** (-0.5))
-        query_sums[here, :] = jnp.where(head_select(256, head), part, query_sums[here, :])
+        here = pl.ds(pl.multiple_of(number * 256, 256), 256)
+        query_sum = jnp.zeros((256, 256), jnp.float32)
+        for head in range(3):
+            query = query_in[here, :]
+            query = jnp.where(head_select(256, head), query, jnp.zeros_like(query))
+            head_grad = grad_out[here, :]
+            head_grad = jnp.where(lane // 64 == head, head_grad, jnp.zeros_like(head_grad))
+            probs = jnp.exp(contract_cols(keys, query) - log_in[head : head + 1, here])
+            delta = jnp.sum(product[head * 64 : (head + 1) * 64, here], 0, keepdims=True)
+            grad_scores = (probs * (contract_cols(values, head_grad) - delta)).astype(jnp.bfloat16)
+            value_sum[...] += dot_nn(probs.astype(jnp.bfloat16), head_grad)
+            key_sum[...] += dot_nn(grad_scores, query)
+            part = dot_nn(key_turned, grad_scores)
+            query_sum = jnp.where((sub % 128) // 32 == head, part, query_sum)
+        query_sums[here, :] = query_sum.T * (HDIM ** (-0.5))
         return carry
 
-    query_sums[...] = jnp.zeros(query_sums.shape, jnp.float32)
-    lax.fori_loop(0, 3 * 4 * block // 256, body, 0)
+    sub = lax.broadcasted_iota(jnp.int32, (256, 1), 0)
+    lax.fori_loop(0, 4 * block // 256, body, 0)
     for j in range(4):
         rows = pl.ds(pl.multiple_of(((j >> 1) + (j & 1) * 2 * stride) * block, 128), block)
         q_part = query_sums[j * block : (j + 1) * block, :]
@@ -596,12 +603,18 @@
 
     @pl.when(step == pl.num_programs(0) - 1)
     def _():
-        summed = total[0:1, :]
-        whole = columns[:, 0:1] * weight_sum[...] + columns[:, 1:2] * summed
-        grad_weight[...] = contract_cols(whole.astype(jnp.bfloat16), chooser[...]).astype(jnp.bfloat16)
-        plain = weight[...].astype(jnp.float32)
-        sums[:, 0:1] = jnp.sum(plain * summed, 1, keepdims=True)
-        sums[:, 1:2] = jnp.sum(plain * weight_sum[...], 1, keepdims=True)
+        def body(i, carry):
+            here = pl.ds(pl.multiple_of(i * 256, 256), 256)
+            summed = total[0:1, :]
+            part = weight_sum[here, :]
+            whole = columns[here, 0:1] * part + columns[here, 1:2] * summed
+            grad_weight[here, :] = contract_cols(whole.astype(jnp.bfloat16), chooser[...]).astype(jnp.bfloat16)
+            plain = weight[here, :].astype(jnp.float32)
+            sums[here, 0:1] = jnp.sum(plain * summed, 1, keepdims=True)
+            sums[here, 1:2] = jnp.sum(plain * part, 1, keepdims=True)
+            return carry
+
+        lax.fori_loop(0, weight.shape[0] // 256, body, 0)
 
 
 def middle_kernel(
@@ -611,15 +624,19 @@
     core = meta[64]
     mine = pl.multiple_of(core * 384, 128)
     theirs = pl.multiple_of(384 - core * 384, 128)
-    for slot in range(16):
-        rows_a = pl.ds(pl.multiple_of(meta[slot] * 48, 16), 48)
-        rows_b = pl.ds(pl.multiple_of(meta[16 + slot] * 48, 16), 48)
-        rows_p = pl.ds(pl.multiple_of(meta[32 + slot] * 48, 16), 48)
-        part_a, part_b, other = (near_a, near_b, other_near) if slot < 8 else (far_a, far_b, other_far)
-        weight_out[rows_a, pl.ds(mine, 256)] = part_a[slot % 8, :, :]
-        weight_out[rows_b, pl.ds(pl.multiple_of(mine + 256, 128), 128)] = part_b[slot % 8, :, :]
-        weight_out[rows_p, pl.ds(theirs, 256)] = other[slot % 8, :, 0:256]
-        weight_out[rows_b, pl.ds(pl.multiple_of(theirs + 256, 128), 128)] = other[slot % 8, :, 256:384]
+    for base, part_a, part_b, other in ((0, near_a, near_b, other_near), (8, far_a, far_b, other_far)):
+
+        def body(slot, carry, base=base, part_a=part_a, part_b=part_b, other=other):
+            rows_a = pl.ds(pl.multiple_of(meta[base + slot] * 48, 16), 48)
+            rows_b = pl.ds(pl.multiple_of(meta[base + slot + 16] * 48, 16), 48)
+            rows_p = pl.ds(pl.multiple_of(meta[base + slot + 32] * 48, 16), 48)
+            weight_out[rows_a, pl.ds(mine, 256)] = part_a[slot]
+            weight_out[rows_b, pl.ds(pl.multiple_of(mine + 256, 128), 128)] = part_b[slot]
+            weight_out[rows_p, pl.ds(theirs, 256)] = other[slot, :, 0:256]
+            weight_out[rows_b, pl.ds(pl.multiple_of(theirs + 256, 128), 128)] = other[slot, :, 256:384]
+            return carry
+
+        lax.fori_loop(0, 8, body, 0)
     projected = dot_nn(attended[...], weight_out[...])
     projected_out[...] = projected
     middle = own_rows[...].astype(jnp.float32) + vectors[3:4, :] * projected
@@ -891,7 +908,7 @@
         project_kernel,
         [((4 * tokens, 256), bf16), ((span, 256), bf16), ((span, 256), bf16), ((span, width), bf16)],
         [meta, x_two, x_far, other_two, other_far, weight_qkv, vectors, cosine, sine],
-        [((8 * tokens, 256), bf16)],
+        [((8 * tokens, 256), bf16), ((chunk, width), bf16)],
         grid=(8,),
         blocks=[(1 + number, part_of(number, width)) for number in range(4)] + [(7, rows_of(128)), (8, rows_of(128))],
         out_blocks=[(1, rows_of(256)), (2, rows_of(256)), (3, rows_of(width))],

time: 305 us -> 307 us (level)
  no operation moved by 1% of the time
where the time goes in v1:
time: 307 us; the launch traced here: 305 us
  Pallas kernels  83.5 us (27%)
  waiting for transfers between devices  78.3 us (26%)
  local copies, waits for them, and re-layouts  60.3 us (20%)
  starting transfers between devices  50.5 us (16%)
  other arithmetic  30.7 us (10%)
    pallas_call x11, Pallas kernels, call(): pl.pallas_call(body, grid=() if grid is None else grid, out_shape=[jax.Sh...  83.5 us
    ppermute x52, waiting for transfers between devices, swap_bits(): lax.ppermute(values, AXES, [(i, i ^ (odd if i & 1 else even)) for i in ra...  78.3 us
    ppermute x52, starting transfers between devices, swap_bits(): lax.ppermute(values, AXES, [(i, i ^ (odd if i & 1 else even)) for i in ra...  50.5 us
    convert_element_type x17, other arithmetic, plus(): return (left.astype(f32) + right.astype(f32)).astype(bf16)  10.4 us
    unnamed x81, local copies, waits for them, and re-layouts  8.9 us
  transfers between devices with their start and end apart: 52, of which 19 were waited for; matrix products, arithmetic and copies ran while one was open for 23% of the time, Pallas kernels for 20%

profile of v1, /device:TPU:0, one launch (start us, length us, event | category | flops | bytes accessed | tf_op | source)
XLA Modules:
  0.0 305.4 jit_solution(3138244215937577010)
XLA Ops:
  1.6 4.1 %collective-permute-start = (bf16[64,768]{1,0:T(8,128)(2,1)S(1)}, bf16[64,768]{1,0:T(8,128)(2,1)S(1)}, u32[]{:S(2)}, u32[]{:S(2)}) collective-permute-start(bf16[64,768]{1,0:T(8,128)(2,1)S(1)} %get-tuple-element.263), channel_id=1, source_target_pairs={{0,8},{1,9},{2,10},{3,11},{4,12},{5,13},{6,14},{7,15},{8,0},{9,1},... | collective-permute-start | bytes 294920 | tf_op jit(solution)/shard_map/ppermute | solution.py:329
  12.6 1.7 shard_map.265
  15.6 4.0 %shard_map.266 = (bf16[432,384]{1,0:T(8,128)(2,1)}, bf16[240,384]{1,0:T(8,128)(2,1)}) custom-call(s32[2]{0:T(128)} %pad_add_fusion.meta, bf16[48,3072]{1,0:T(8,128)(2,1)} %w_in, bf16[48,768]{1,0:T(8,128)(2,1)} %w_out, bf16[192,768]{1,0:T(8,128)(2,1)} %w_down), custom_call_target="tpu_custom_call" | custom-call | tf_op jit(solution)/shard_map/pallas_call | solution.py:756
  19.7 1.6 collective-permute-start.1
  23.7 4.0 %collective-permute-done.1 = bf16[128,768]{1,0:T(8,128)(2,1)S(1)} collective-permute-done((bf16[128,768]{1,0:T(8,128)(2,1)S(1)}, bf16[128,768]{1,0:T(8,128)(2,1)S(1)}, u32[]{:S(2)}, u32[]{:S(2)}) %collective-permute-start.1) | collective-permute-done | bytes 196640 | tf_op jit(solution)/shard_map/ppermute | solution.py:329
  27.8 1.8 collective-permute-start.3
  31.9 2.8 collective-permute-start.7
  34.7 1.6 multiply_add_fusion
  38.0 7.0 %collective-permute-done.4 = bf16[208,576]{1,0:T(8,128)(2,1)S(1)} collective-permute-done((bf16[208,576]{1,0:T(8,128)(2,1)S(1)}, bf16[208,576]{1,0:T(8,128)(2,1)S(1)}, u32[]{:S(2)}, u32[]{:S(2)}) %collective-permute-start.4) | collective-permute-done | bytes 239648 | tf_op jit(solution)/shard_map/ppermute | solution.py:329
  45.2 1.6 collective-permute-start.6
  48.3 3.3 %collective-permute-done.7 = bf16[432,384]{1,0:T(8,128)(2,1)S(1)} collective-permute-done((bf16[432,384]{1,0:T(8,128)(2,1)S(1)}, bf16[432,384]{1,0:T(8,128)(2,1)S(1)}, u32[]{:S(2)}, u32[]{:S(2)}) %collective-permute-start.7) | collective-permute-done | bytes 331808 | tf_op jit(solution)/shard_map/ppermute | solution.py:329
  51.6 2.8 collective-permute-done.6
  56.3 2.1 collective-permute-start.8
  58.4 5.1 %collective-permute-done.10 = bf16[1,2,432,128]{3,2,1,0:T(8,128)(2,1)S(1)} collective-permute-done((bf16[1,2,432,128]{3,2,1,0:T(8,128)(2,1)S(1)}, bf16[1,2,432,128]{3,2,1,0:T(8,128)(2,1)S(1)}, u32[]{:S(2)}, u32[]{:S(2)}) %collective-permute-start.10) | collective-permute-done | bytes 221216 | tf_op jit(solution)/shard_map/ppermute | solution.py:329
  63.7 3.4 %collective-permute-done.8 = bf16[256,576]{1,0:T(8,128)(2,1)S(1)} collective-permute-done((bf16[256,576]{1,0:T(8,128)(2,1)S(1)}, bf16[256,576]{1,0:T(8,128)(2,1)S(1)}, u32[]{:S(2)}, u32[]{:S(2)}) %collective-permute-start.8) | collective-permute-done | bytes 294944 | tf_op jit(solution)/shard_map/ppermute | solution.py:329
  80.1 3.9 %shard_map.267.weight = bf16[768,768]{1,0:T(8,128)(2,1)} custom-call(s32[65]{0:T(128)} %concatenate.150.meta, bf16[512,576]{1,0:T(8,128)(2,1)} %copy-done, bf16[512,576]{1,0:T(8,128)(2,1)} %copy.104.other, bf16[576,768]{1,0:T(8,128)(2,1)} %fusion.chooser), custom_call_target="tpu_custom_call" | custom-call | flops 679477248 | bytes 3000000 | tf_op jit(solution)/shard_map/pallas_call | solution.py:756
  84.0 11.2 %shard_map.268 = (bf16[512,256]{1,0:T(8,128)(2,1)}, bf16[2048,256]{1,0:T(8,128)(2,1)}, bf16[2048,256]{1,0:T(8,128)(2,1)}, bf16[2048,768]{1,0:T(8,128)(2,1)}) custom-call(s32[65]{0:T(128)} %concatenate.150.meta, bf16[512,768]{1,0:T(8,128)(2,1)} %pad_maximum_fusion.2.near, bf16[512,768]{1,0:T(8,128)(2,1)} %copy-done.33, ...), custom_call_target="tpu_custom_call" | custom-call | flops 2000000000 | bytes 8000000 | tf_op jit(solution)/shard_map/pallas_call | solution.py:756
  95.2 2.2 constant_dynamic-update-slice_fusion.7
  101.4 1.8 constant_dynamic-update-slice_fusion.9
  104.7 10.9 %shard_map.269 = (f32[256,512]{1,0:T(8,128)}, f32[8,512]{1,0:T(8,128)}, bf16[4,128,192]{2,1,0:T(8,128)(2,1)}) custom-call(s32[65]{0:T(128)} %concatenate.150.meta, bf16[512,256]{1,0:T(8,128)(2,1)} %get-tuple-element.131.query_in, bf16[2048,256]{1,0:T(8,128)(2,1)} %get-tuple-element.135.key_in, bf16[2048,256]{1,0:T(8,128)(2,1)} %get-tuple-element.136.value_in), custom_call_target="tpu_custom_call" | custom-call | flops 8000000000 | bytes 4000000 | tf_op jit(solution)/shard_map/pallas_call | solution.py:756
  119.3 8.6 %collective-permute-done.16 = bf16[2,128,192]{2,1,0:T(8,128)(2,1)S(1)} collective-permute-done((bf16[2,128,192]{2,1,0:T(8,128)(2,1)S(1)}, bf16[2,128,192]{2,1,0:T(8,128)(2,1)S(1)}, u32[]{:S(2)}, u32[]{:S(2)}) %collective-permute-start.16) | collective-permute-done | bytes 98336 | tf_op jit(solution)/shard_map/ppermute | solution.py:329
  131.3 1.7 collective-permute-done.19
  136.2 3.4 %shard_map.270 = (f32[128,768]{1,0:T(8,128)}, f32[128,768]{1,0:T(8,128)}, bf16[128,768]{1,0:T(8,128)(2,1)}, bf16[768,768]{1,0:T(8,128)(2,1)}) custom-call(s32[65]{0:T(128)} %concatenate.150.meta, bf16[128,768]{1,0:T(8,128)(2,1)} %copy.113.attended, bf16[8,48,256]{2,1,0:T(8,128)(2,1)} %copy-done.2, bf16[8,48,128]{2,1,0:T(8,128)(2,1)} %copy-done.10, ...), custom_call_target="tpu_custom_call" | custom-call | flops 150000000 | bytes 3000000 | tf_op jit(solution)/shard_map/pallas_call | solution.py:756
  142.0 13.4 %shard_map.271 = (f32[2,128,768]{2,1,0:T(8,128)}, f32[2,128,768]{2,1,0:T(8,128)}, bf16[8,384,256]{2,1,0:T(8,128)(2,1)}, bf16[8,384,128]{2,1,0:T(8,128)(2,1)}, bf...) custom-call(s32[65]{0:T(128)} %concatenate.150.meta, ...), custom_call_target="tpu_custom_call" | custom-call | flops 3600000000 | bytes 12000000 | tf_op jit(solution)/shard_map/pallas_call | solution.py:756
  158.9 4.3 %shard_map.272 = (bf16[128,768]{1,0:T(8,128)(2,1)}, f32[128,768]{1,0:T(8,128)}, bf16[128,768]{1,0:T(8,128)(2,1)}, bf16[768,768]{1,0:T(8,128)(2,1)}, f32[8,768]{1,0:T(8,128)}) custom-call(s32[65]{0:T(128)} %concatenate.150.meta, f32[2,128,768]{2,1,0:T(8,128)} %get-tuple-element.147.sums_own, f32[2,128,768]{2,1,0:T(8,128)} %copy-done.13, ...), custom_call_target="tpu_custom_call" | custom-call | flops 300000000 | bytes 5000000 | tf_op jit(solution)/shard_map/pallas_call | solution.py:756
  166.6 3.8 %collective-permute-done.26 = bf16[2,128,192]{1,2,0:T(8,128)(2,1)S(1)} collective-permute-done((bf16[2,128,192]{1,2,0:T(8,128)(2,1)S(1)}, bf16[2,128,192]{1,2,0:T(8,128)(2,1)S(1)}, u32[]{:S(2)}, u32[]{:S(2)}) %collective-permute-start.26) | collective-permute-done | bytes 98336 | tf_op jit(solution)/shard_map/ppermute | solution.py:329
  173.8 2.2 collective-permute-done.27
  177.9 14.0 %shard_map.273 = (bf16[512,256]{1,0:T(8,128)(2,1)}, f32[2048,256]{1,0:T(8,128)}, f32[2048,256]{1,0:T(8,128)}) custom-call(s32[65]{0:T(128)} %concatenate.150.meta, f32[2048,128]{1,0:T(8,128)} %bitcast.308, f32[2048,128]{1,0:T(8,128)} %bitcast.305, bf16[512,256]{1,0:T(8,128)(2,1)} %get-tuple-element.131.query_in, ...), custom_call_target="tpu_custom_call" | custom-call | flops 14000000000 | bytes 8000000 | tf_op jit(solution)/shard_map/pallas_call | solution.py:756
  191.9 1.8 maximum_select_fusion.3
  194.9 1.8 add_convert_fusion
  197.8 2.5 collective-permute-start.32
  204.9 14.5 %shard_map.274 = (bf16[1024,768]{1,0:T(8,128)(2,1)}, bf16[1024,768]{1,0:T(8,128)(2,1)}, bf16[768,576]{1,0:T(8,128)(2,1)}, f32[768,2]{1,0:T(8,128)}) custom-call(s32[65]{0:T(128)} %concatenate.150.meta, bf16[2048,768]{1,0:T(8,128)(2,1)} %get-tuple-element.162.norm, bf16[768,768]{1,0:T(8,128)(2,1)} %shard_map.267.weight, bf16[576,768]{1,0:T(8,128)(2,1)} %fusion.chooser, ...), custom_call_target="tpu_custom_call" | custom-call | flops 6000000000 | bytes 16000000 | tf_op jit(solution)/shard_map/pallas_call | solution.py:756
  223.8 1.6 collective-permute-start.38
  228.8 4.0 %collective-permute-done.39 = bf16[768,128]{1,0:T(8,128)(2,1)S(1)} collective-permute-done((bf16[768,128]{1,0:T(8,128)(2,1)S(1)}, bf16[768,128]{1,0:T(8,128)(2,1)S(1)}, u32[]{:S(2)}, u32[]{:S(2)}) %collective-permute-start.39) | collective-permute-done | bytes 196640 | tf_op jit(solution)/shard_map/ppermute | solution.py:329
  232.9 1.8 fusion.3
  236.2 1.6 collective-permute-start.41
  238.3 6.8 %collective-permute-done.41 = bf16[2,2,48,576]{3,2,0,1:T(8,128)(2,1)S(1)} collective-permute-done((bf16[2,2,48,576]{3,2,0,1:T(8,128)(2,1)S(1)}, bf16[2,2,48,576]{3,2,0,1:T(8,128)(2,1)S(1)}, u32[]{:S(2)}, u32[]{:S(2)}) %collective-permute-start.41) | collective-permute-done | bytes 221216 | tf_op jit(solution)/shard_map/ppermute | solution.py:329
  245.1 2.2 collective-permute-done.40
  247.4 4.9 %collective-permute-done.42 = bf16[384,384]{1,0:T(8,128)(2,1)S(1)} collective-permute-done((bf16[384,384]{1,0:T(8,128)(2,1)S(1)}, bf16[384,384]{1,0:T(8,128)(2,1)S(1)}, u32[]{:S(2)}, u32[]{:S(2)}) %collective-permute-start.42) | collective-permute-done | bytes 294944 | tf_op jit(solution)/shard_map/ppermute | solution.py:329
  255.2 1.8 collective-permute-start.45
  257.0 7.8 %collective-permute-done.44 = bf16[192,960]{1,0:T(8,128)(2,1)S(1)} collective-permute-done((bf16[192,960]{1,0:T(8,128)(2,1)S(1)}, bf16[192,960]{1,0:T(8,128)(2,1)S(1)}, u32[]{:S(2)}, u32[]{:S(2)}) %collective-permute-start.44) | collective-permute-done | bytes 368672 | tf_op jit(solution)/shard_map/ppermute | solution.py:329
  270.4 1.8 collective-permute-start.46
  274.9 6.6 %collective-permute-done.46 = bf16[160,768]{1,0:T(8,128)(2,1)S(1)} collective-permute-done((bf16[160,768]{1,0:T(8,128)(2,1)S(1)}, bf16[160,768]{1,0:T(8,128)(2,1)S(1)}, u32[]{:S(2)}, u32[]{:S(2)}) %collective-permute-start.46) | collective-permute-done | bytes 245792 | tf_op jit(solution)/shard_map/ppermute | solution.py:329
  282.2 3.5 %collective-permute-start.49 = (f32[9,768]{1,0:T(8,128)S(1)}, f32[9,768]{1,0:T(8,128)S(1)}, u32[]{:S(2)}, u32[]{:S(2)}) collective-permute-start(f32[9,768]{1,0:T(8,128)S(1)} %convert_add_fusion.14), channel_id=1, source_target_pairs={{0,8},{1,9},{2,10},{3,11},{4,12},{5,13},{6,14},{7,15},{8,0},{9,1},... | collective-permute-start | bytes 82952 | tf_op jit(solution)/shard_map/ppermute | solution.py:329
  285.7 2.3 shard_map.275
  289.0 1.6 reshape.1167
  295.8 2.3 collective-permute-start.51
  302.1 1.8 collective-permute-done.51
  (387 shorter events, 101.8 us)
Async XLA Ops:
  1.6 14.0 %collective-permute-start = (bf16[64,768]{1,0:T(8,128)(2,1)S(1)}, bf16[64,768]{1,0:T(8,128)(2,1)S(1)}, u32[]{:S(2)}, u32[]{:S(2)}) collective-permute-start(bf16[64,768]{1,0:T(8,128)(2,1)S(1)} %get-tuple-element.263), channel_id=1, source_target_pairs={{0,8},{1,9},{2,10},{3,11},{4,12},{5,13},{6,14},{7,15},{8,0},{9,1},... | collective-permute-start | bytes 294920 | tf_op jit(solution)/shard_map/ppermute | solution.py:329
  19.7 8.0 %collective-permute-start.1 = (bf16[128,768]{1,0:T(8,128)(2,1)S(1)}, bf16[128,768]{1,0:T(8,128)(2,1)S(1)}, u32[]{:S(2)}, u32[]{:S(2)}) collective-permute-start(bf16[128,768]{1,0:T(8,128)(2,1)S(1)} %pad_maximum_fusion.22.own_rows.source), channel_id=1, source_target_pairs={{0,4},{1,5},{2,6},{3,7},{4,0},{5,1},{6,2},{7,3},{8,12},{9,13},{10,... | collective-permute-start | bytes 589832 | tf_op jit(solution)/shard_map/ppermute | solution.py:329
  22.2 22.8 %collective-permute-start.4 = (bf16[208,576]{1,0:T(8,128)(2,1)S(1)}, bf16[208,576]{1,0:T(8,128)(2,1)S(1)}, u32[]{:S(2)}, u32[]{:S(2)}) collective-permute-start(bf16[208,576]{1,0:T(8,128)(2,1)S(1)} %pad_maximum_fusion.17), channel_id=1, source_target_pairs={{0,8},{1,9},{2,10},{3,11},{4,12},{5,13},{6,14},{7,15},{8,0},{9,1},... | collective-permute-start | bytes 718856 | tf_op jit(solution)/shard_map/ppermute | solution.py:329
  27.8 9.2 %collective-permute-start.3 = (bf16[256,768]{1,0:T(8,128)(2,1)S(1)}, bf16[256,768]{1,0:T(8,128)(2,1)S(1)}, u32[]{:S(2)}, u32[]{:S(2)}) collective-permute-start(bf16[256,768]{1,0:T(8,128)(2,1)S(1)} %pad_maximum_fusion.7), channel_id=1, source_target_pairs={{0,2},{1,17},{2,0},{3,19},{4,6},{5,21},{6,4},{7,23},{8,10},{9,25},... | collective-permute-start | bytes 1179656 | tf_op jit(solution)/shard_map/ppermute | solution.py:329
  31.9 19.7 %collective-permute-start.7 = (bf16[432,384]{1,0:T(8,128)(2,1)S(1)}, bf16[432,384]{1,0:T(8,128)(2,1)S(1)}, u32[]{:S(2)}, u32[]{:S(2)}) collective-permute-start(bf16[432,384]{1,0:T(8,128)(2,1)S(1)} %pad_maximum_fusion.9), channel_id=1, source_target_pairs={{0,8},{1,9},{2,10},{3,11},{4,12},{5,13},{6,14},{7,15},{8,0},{9,1},... | collective-permute-start | bytes 995336 | tf_op jit(solution)/shard_map/ppermute | solution.py:329
  45.2 9.2 %collective-permute-start.6 = (bf16[224,576]{1,0:T(8,128)(2,1)S(1)}, bf16[224,576]{1,0:T(8,128)(2,1)S(1)}, u32[]{:S(2)}, u32[]{:S(2)}) collective-permute-start(bf16[224,576]{1,0:T(8,128)(2,1)S(1)} %pad_maximum_fusion.16), channel_id=1, source_target_pairs={{0,2},{1,3},{2,0},{3,1},{4,6},{5,7},{6,4},{7,5},{8,10},{9,11},{10,... | collective-permute-start | bytes 774152 | tf_op jit(solution)/shard_map/ppermute | solution.py:329
  46.8 20.2 %collective-permute-start.5 = (bf16[512,768]{1,0:T(8,128)(2,1)}, bf16[512,768]{1,0:T(8,128)(2,1)S(1)}, u32[]{:S(2)}, u32[]{:S(2)}) collective-permute-start(bf16[512,768]{1,0:T(8,128)(2,1)} %pad_maximum_fusion.2.near), channel_id=1, source_target_pairs={{0,16},{1,3},{2,18},{3,1},{4,20},{5,7},{6,22},{7,5},{8,24},{9,11},... | collective-permute-start | bytes 2359304 | tf_op jit(solution)/shard_map/ppermute | solution.py:329
  54.6 9.0 %collective-permute-start.9 = (bf16[1,2,432,256]{3,2,1,0:T(8,128)(2,1)S(1)}, bf16[1,2,432,256]{3,2,1,0:T(8,128)(2,1)S(1)}, u32[]{:S(2)}, u32[]{:S(2)}) collective-permute-start(bf16[1,2,432,256]{3,2,1,0:T(8,128)(2,1)S(1)} %slice.434), channel_id=1, source_target_pairs={{0,2},{1,17},{2,0},{3,19},{4,6},{5,21},{6,4},{7,23},{8,10},{9,25},... | collective-permute-start | bytes 1327112 | tf_op jit(solution)/shard_map/ppermute | solution.py:329
  56.1 7.4 %collective-permute-start.10 = (bf16[1,2,432,128]{3,2,1,0:T(8,128)(2,1)S(1)}, bf16[1,2,432,128]{3,2,1,0:T(8,128)(2,1)S(1)}, u32[]{:S(2)}, u32[]{:S(2)}) collective-permute-start(bf16[1,2,432,128]{3,2,1,0:T(8,128)(2,1)S(1)} %slice.435), channel_id=1, source_target_pairs={{0,4},{1,5},{2,6},{3,7},{4,0},{5,1},{6,2},{7,3},{8,12},{9,13},{10,... | collective-permute-start | bytes 663560 | tf_op jit(solution)/shard_map/ppermute | solution.py:329
  56.3 10.8 %collective-permute-start.8 = (bf16[256,576]{1,0:T(8,128)(2,1)S(1)}, bf16[256,576]{1,0:T(8,128)(2,1)S(1)}, u32[]{:S(2)}, u32[]{:S(2)}) collective-permute-start(bf16[256,576]{1,0:T(8,128)(2,1)S(1)} %pad_maximum_fusion.10), channel_id=1, source_target_pairs={{0,4},{1,5},{2,6},{3,7},{4,0},{5,1},{6,2},{7,3},{8,12},{9,13},{10,... | collective-permute-start | bytes 884744 | tf_op jit(solution)/shard_map/ppermute | solution.py:329
  68.2 5.0 %collective-permute-start.13 = (bf16[512,576]{0,1:T(8,128)(2,1)S(1)}, bf16[512,576]{0,1:T(8,128)(2,1)S(1)}, u32[]{:S(2)}, u32[]{:S(2)}) collective-permute-start(bf16[512,576]{0,1:T(8,128)(2,1)S(1)} %copy.103), channel_id=1, source_target_pairs={{0,1},{1,0},{2,3},{3,2},{4,5},{5,4},{6,7},{7,6},{8,9},{9,8},{10,11... | collective-permute-start | bytes 1769480 | tf_op jit(solution)/shard_map/ppermute | solution.py:329
  68.3 15.7 %collective-permute-start.11 = (bf16[512,768]{1,0:T(8,128)(2,1)}, bf16[512,768]{1,0:T(8,128)(2,1)}, u32[]{:S(2)}, u32[]{:S(2)}) collective-permute-start(bf16[512,768]{1,0:T(8,128)(2,1)} %pad_maximum_fusion.2.near), channel_id=1, source_target_pairs={{0,1},{1,0},{2,3},{3,2},{4,5},{5,4},{6,7},{7,6},{8,9},{9,8},{10,11... | collective-permute-start | bytes 2359304 | tf_op jit(solution)/shard_map/ppermute | solution.py:329
  70.6 13.5 %collective-permute-start.12 = (bf16[512,768]{1,0:T(8,128)(2,1)}, bf16[512,768]{1,0:T(8,128)(2,1)}, u32[]{:S(2)}, u32[]{:S(2)}) collective-permute-start(bf16[512,768]{1,0:T(8,128)(2,1)} %copy-done.33), channel_id=1, source_target_pairs={{0,1},{1,0},{2,3},{3,2},{4,5},{5,4},{6,7},{7,6},{8,9},{9,8},{10,11... | collective-permute-start | bytes 2359304 | tf_op jit(solution)/shard_map/ppermute | solution.py:329
  71.4 23.8 %collective-permute-start.14 = (bf16[2,2,432,256]{3,2,1,0:T(8,128)(2,1)S(1)}, bf16[2,2,432,256]{3,2,1,0:T(8,128)(2,1)}, u32[]{:S(2)}, u32[]{:S(2)}) collective-permute-start(bf16[2,2,432,256]{3,2,1,0:T(8,128)(2,1)S(1)} %pad_maximum_fusion), channel_id=1, source_target_pairs={{0,4},{1,3},{2,6},{3,1},{4,0},{5,7},{6,2},{7,5},{8,12},{9,11},{10,... | collective-permute-start | bytes 2654216 | tf_op jit(solution)/shard_map/ppermute | solution.py:329
  71.7 23.5 %collective-permute-start.15 = (bf16[2,2,432,128]{3,2,1,0:T(8,128)(2,1)S(1)}, bf16[2,2,432,128]{3,2,1,0:T(8,128)(2,1)}, u32[]{:S(2)}, u32[]{:S(2)}) collective-permute-start(bf16[2,2,432,128]{3,2,1,0:T(8,128)(2,1)S(1)} %pad_maximum_fusion.5), channel_id=1, source_target_pairs={{0,16},{1,17},{2,18},{3,19},{4,20},{5,21},{6,22},{7,23},{8,24},{9,... | collective-permute-start | bytes 1327112 | tf_op jit(solution)/shard_map/ppermute | solution.py:329
  97.4 30.5 %collective-permute-start.17 = (bf16[4,2,432,256]{3,2,1,0:T(8,128)(2,1)}, bf16[4,2,432,256]{3,2,1,0:T(8,128)(2,1)}, u32[]{:S(2)}, u32[]{:S(2)}) collective-permute-start(bf16[4,2,432,256]{3,2,1,0:T(8,128)(2,1)} %constant_dynamic-update-slice_fusion.7), channel_id=1, source_target_pairs={{0,16},{1,5},{2,18},{3,7},{4,20},{5,1},{6,22},{7,3},{8,24},{9,13},... | collective-permute-start | bytes 5308424 | tf_op jit(solution)/shard_map/ppermute | solution.py:329
  99.6 31.0 %collective-permute-start.23 = (bf16[64,768]{1,0:T(8,128)(2,1)}, bf16[64,768]{1,0:T(8,128)(2,1)S(1)}, u32[]{:S(2)}, u32[]{:S(2)}) collective-permute-start(bf16[64,768]{1,0:T(8,128)(2,1)} %get-tuple-element.261), channel_id=1, source_target_pairs={{0,8},{1,9},{2,10},{3,11},{4,12},{5,13},{6,14},{7,15},{8,0},{9,1},... | collective-permute-start | bytes 294920 | tf_op jit(solution)/shard_map/ppermute | solution.py:329
  103.2 24.7 %collective-permute-start.18 = (bf16[4,2,432,128]{3,2,1,0:T(8,128)(2,1)}, bf16[4,2,432,128]{3,2,1,0:T(8,128)(2,1)}, u32[]{:S(2)}, u32[]{:S(2)}) collective-permute-start(bf16[4,2,432,128]{3,2,1,0:T(8,128)(2,1)} %constant_dynamic-update-slice_fusion.9), channel_id=1, source_target_pairs={{0,2},{1,3},{2,0},{3,1},{4,6},{5,7},{6,4},{7,5},{8,10},{9,11},{10,... | collective-permute-start | bytes 2654216 | tf_op jit(solution)/shard_map/ppermute | solution.py:329
  116.6 11.3 %collective-permute-start.16 = (bf16[2,128,192]{2,1,0:T(8,128)(2,1)S(1)}, bf16[2,128,192]{2,1,0:T(8,128)(2,1)S(1)}, u32[]{:S(2)}, u32[]{:S(2)}) collective-permute-start(bf16[2,128,192]{2,1,0:T(8,128)(2,1)S(1)} %get-tuple-element.253), channel_id=1, source_target_pairs={{0,2},{1,3},{2,0},{3,1},{4,6},{5,7},{6,4},{7,5},{8,10},{9,11},{10,... | collective-permute-start | bytes 294920 | tf_op jit(solution)/shard_map/ppermute | solution.py:329
  119.2 15.6 %collective-permute-start.20 = (bf16[8,48,384]{2,1,0:T(8,128)(2,1)S(1)}, bf16[8,48,384]{2,1,0:T(8,128)(2,1)S(1)}, u32[]{:S(2)}, u32[]{:S(2)}) collective-permute-start(bf16[8,48,384]{2,1,0:T(8,128)(2,1)S(1)} %pad_maximum_fusion.12), channel_id=1, source_target_pairs={{0,1},{1,0},{2,3},{3,2},{4,5},{5,4},{6,7},{7,6},{8,9},{9,8},{10,11... | collective-permute-start | bytes 884744 | tf_op jit(solution)/shard_map/ppermute | solution.py:329
  128.0 5.0 %collective-permute-start.19 = (bf16[2,128,192]{2,1,0:T(8,128)(2,1)S(1)}, bf16[2,128,192]{2,1,0:T(8,128)(2,1)S(1)}, u32[]{:S(2)}, u32[]{:S(2)}) collective-permute-start(bf16[2,128,192]{2,1,0:T(8,128)(2,1)S(1)} %get-tuple-element.251), channel_id=1, source_target_pairs={{0,4},{1,5},{2,6},{3,7},{4,0},{5,1},{6,2},{7,3},{8,12},{9,13},{10,... | collective-permute-start | bytes 294920 | tf_op jit(solution)/shard_map/ppermute | solution.py:329
  130.7 10.6 %collective-permute-start.24 = (bf16[128,768]{1,0:T(8,128)(2,1)S(1)}, bf16[128,768]{1,0:T(8,128)(2,1)}, u32[]{:S(2)}, u32[]{:S(2)}) collective-permute-start(bf16[128,768]{1,0:T(8,128)(2,1)S(1)} %multiply_convert_fusion.grad_own.grad_branch), channel_id=1, source_target_pairs={{0,1},{1,0},{2,3},{3,2},{4,5},{5,4},{6,7},{7,6},{8,9},{9,8},{10,11... | collective-permute-start | bytes 589832 | tf_op jit(solution)/shard_map/ppermute | solution.py:329
  165.2 5.1 %collective-permute-start.26 = (bf16[2,128,192]{1,2,0:T(8,128)(2,1)S(1)}, bf16[2,128,192]{1,2,0:T(8,128)(2,1)S(1)}, u32[]{:S(2)}, u32[]{:S(2)}) collective-permute-start(bf16[2,128,192]{1,2,0:T(8,128)(2,1)S(1)} %get-tuple-element.259), channel_id=1, source_target_pairs={{0,2},{1,3},{2,0},{3,1},{4,6},{5,7},{6,4},{7,5},{8,10},{9,11},{10,... | collective-permute-start | bytes 294920 | tf_op jit(solution)/shard_map/ppermute | solution.py:329
  170.4 5.7 %collective-permute-start.27 = (bf16[2,128,192]{1,2,0:T(8,128)(2,1)S(1)}, bf16[2,128,192]{1,2,0:T(8,128)(2,1)S(1)}, u32[]{:S(2)}, u32[]{:S(2)}) collective-permute-start(bf16[2,128,192]{1,2,0:T(8,128)(2,1)S(1)} %get-tuple-element.257), channel_id=1, source_target_pairs={{0,4},{1,5},{2,6},{3,7},{4,0},{5,1},{6,2},{7,3},{8,12},{9,13},{10,... | collective-permute-start | bytes 294920 | tf_op jit(solution)/shard_map/ppermute | solution.py:329
  172.0 22.9 %collective-permute-start.28 = (bf16[8,384,256]{2,1,0:T(8,128)(2,1)}, bf16[8,384,256]{2,1,0:T(8,128)(2,1)}, u32[]{:S(2)}, u32[]{:S(2)}) collective-permute-start(bf16[8,384,256]{2,1,0:T(8,128)(2,1)} %get-tuple-element.157), channel_id=1, source_target_pairs={{0,16},{1,5},{2,18},{3,7},{4,20},{5,1},{6,22},{7,3},{8,24},{9,13},... | collective-permute-start | bytes 4718600 | tf_op jit(solution)/shard_map/ppermute | solution.py:329
  173.3 21.6 %collective-permute-start.29 = (bf16[8,384,128]{2,1,0:T(8,128)(2,1)}, bf16[8,384,128]{2,1,0:T(8,128)(2,1)}, u32[]{:S(2)}, u32[]{:S(2)}) collective-permute-start(bf16[8,384,128]{2,1,0:T(8,128)(2,1)} %get-tuple-element.158), channel_id=1, source_target_pairs={{0,2},{1,3},{2,0},{3,1},{4,6},{5,7},{6,4},{7,5},{8,10},{9,11},{10,... | collective-permute-start | bytes 2359304 | tf_op jit(solution)/shard_map/ppermute | solution.py:329
  176.9 16.7 %collective-permute-start.30 = (bf16[8,48,768]{2,1,0:T(8,128)(2,1)S(1)}, bf16[8,48,768]{2,1,0:T(8,128)(2,1)}, u32[]{:S(2)}, u32[]{:S(2)}) collective-permute-start(bf16[8,48,768]{2,1,0:T(8,128)(2,1)S(1)} %dynamic-slice_bitcast_fusion), channel_id=1, source_target_pairs={{0,1},{1,0},{2,3},{3,2},{4,5},{5,4},{6,7},{7,6},{8,9},{9,8},{10,11... | collective-permute-start | bytes 1769480 | tf_op jit(solution)/shard_map/ppermute | solution.py:329
  177.1 14.9 %collective-permute-start.31 = (bf16[64,768]{1,0:T(8,128)(2,1)S(1)}, bf16[64,768]{1,0:T(8,128)(2,1)}, u32[]{:S(2)}, u32[]{:S(2)}) collective-permute-start(bf16[64,768]{1,0:T(8,128)(2,1)S(1)} %get-tuple-element.255), channel_id=1, source_target_pairs={{0,8},{1,9},{2,10},{3,11},{4,12},{5,13},{6,14},{7,15},{8,0},{9,1},... | collective-permute-start | bytes 294920 | tf_op jit(solution)/shard_map/ppermute | solution.py:329
  197.8 21.7 %collective-permute-start.32 = (bf16[2,768,256]{2,1,0:T(8,128)(2,1)}, bf16[2,768,256]{2,1,0:T(8,128)(2,1)}, u32[]{:S(2)}, u32[]{:S(2)}) collective-permute-start(bf16[2,768,256]{2,1,0:T(8,128)(2,1)} %bitcast.89), channel_id=1, source_target_pairs={{0,4},{1,3},{2,6},{3,1},{4,0},{5,7},{6,2},{7,5},{8,12},{9,11},{10,... | collective-permute-start | bytes 2359304 | tf_op jit(solution)/shard_map/ppermute | solution.py:329
  202.4 17.1 %collective-permute-start.33 = (bf16[2,768,128]{2,1,0:T(8,128)(2,1)}, bf16[2,768,128]{2,1,0:T(8,128)(2,1)}, u32[]{:S(2)}, u32[]{:S(2)}) collective-permute-start(bf16[2,768,128]{2,1,0:T(8,128)(2,1)} %bitcast.90), channel_id=1, source_target_pairs={{0,16},{1,17},{2,18},{3,19},{4,20},{5,21},{6,22},{7,23},{8,24},{9,... | collective-permute-start | bytes 1179656 | tf_op jit(solution)/shard_map/ppermute | solution.py:329
  204.4 15.1 %collective-permute-start.34 = (bf16[2,2,48,768]{3,2,1,0:T(8,128)(2,1)}, bf16[2,2,48,768]{3,2,1,0:T(8,128)(2,1)}, u32[]{:S(2)}, u32[]{:S(2)}) collective-permute-start(bf16[2,2,48,768]{3,2,1,0:T(8,128)(2,1)} %dynamic-slice_bitcast_fusion.2), channel_id=1, source_target_pairs={{0,2},{1,3},{2,0},{3,1},{4,6},{5,7},{6,4},{7,5},{8,10},{9,11},{10,... | collective-permute-start | bytes 884744 | tf_op jit(solution)/shard_map/ppermute | solution.py:329
  219.5 13.4 %collective-permute-start.35 = (bf16[1024,768]{1,0:T(8,128)(2,1)}, bf16[1024,768]{1,0:T(8,128)(2,1)}, u32[]{:S(2)}, u32[]{:S(2)}) collective-permute-start(bf16[1024,768]{1,0:T(8,128)(2,1)} %get-tuple-element.176), channel_id=1, source_target_pairs={{0,1},{1,0},{2,3},{3,2},{4,5},{5,4},{6,7},{7,6},{8,9},{9,8},{10,11... | collective-permute-start | bytes 4718600 | tf_op jit(solution)/shard_map/ppermute | solution.py:329
  220.7 7.9 %collective-permute-start.36 = (f32[7,768]{1,0:T(8,128)S(1)}, f32[7,768]{1,0:T(8,128)S(1)}, u32[]{:S(2)}, u32[]{:S(2)}) collective-permute-start(f32[7,768]{1,0:T(8,128)S(1)} %pad_maximum_fusion.28), channel_id=1, source_target_pairs={{0,1},{1,0},{2,3},{3,2},{4,5},{5,4},{6,7},{7,6},{8,9},{9,8},{10,11... | collective-permute-start | bytes 64520 | tf_op jit(solution)/shard_map/ppermute | solution.py:329
  222.4 6.3 %collective-permute-start.37 = (bf16[8,48,576]{2,1,0:T(8,128)(2,1)S(1)}, bf16[8,48,576]{2,1,0:T(8,128)(2,1)S(1)}, u32[]{:S(2)}, u32[]{:S(2)}) collective-permute-start(bf16[8,48,576]{2,1,0:T(8,128)(2,1)S(1)} %dynamic-slice_bitcast_fusion.1), channel_id=1, source_target_pairs={{0,1},{1,0},{2,3},{3,2},{4,5},{5,4},{6,7},{7,6},{8,9},{9,8},{10,11... | collective-permute-start | bytes 1327112 | tf_op jit(solution)/shard_map/ppermute | solution.py:329
  223.8 9.1 %collective-permute-start.38 = (bf16[768,256]{1,0:T(8,128)(2,1)S(1)}, bf16[768,256]{1,0:T(8,128)(2,1)S(1)}, u32[]{:S(2)}, u32[]{:S(2)}) collective-permute-start(bf16[768,256]{1,0:T(8,128)(2,1)S(1)} %slice_bitcast_fusion.1), channel_id=1, source_target_pairs={{0,2},{1,17},{2,0},{3,19},{4,6},{5,21},{6,4},{7,23},{8,10},{9,25},... | collective-permute-start | bytes 1179656 | tf_op jit(solution)/shard_map/ppermute | solution.py:329
  226.5 6.3 %collective-permute-start.39 = (bf16[768,128]{1,0:T(8,128)(2,1)S(1)}, bf16[768,128]{1,0:T(8,128)(2,1)S(1)}, u32[]{:S(2)}, u32[]{:S(2)}) collective-permute-start(bf16[768,128]{1,0:T(8,128)(2,1)S(1)} %slice_bitcast_fusion.4), channel_id=1, source_target_pairs={{0,4},{1,5},{2,6},{3,7},{4,0},{5,1},{6,2},{7,3},{8,12},{9,13},{10,... | collective-permute-start | bytes 589832 | tf_op jit(solution)/shard_map/ppermute | solution.py:329
  234.8 12.6 %collective-permute-start.40 = (bf16[544,768]{1,0:T(8,128)(2,1)S(1)}, bf16[544,768]{1,0:T(8,128)(2,1)S(1)}, u32[]{:S(2)}, u32[]{:S(2)}) collective-permute-start(bf16[544,768]{1,0:T(8,128)(2,1)S(1)} %pad_maximum_fusion.1), channel_id=1, source_target_pairs={{0,16},{1,3},{2,18},{3,1},{4,20},{5,7},{6,22},{7,5},{8,24},{9,11},... | collective-permute-start | bytes 2506760 | tf_op jit(solution)/shard_map/ppermute | solution.py:329
  236.2 8.9 %collective-permute-start.41 = (bf16[2,2,48,576]{3,2,0,1:T(8,128)(2,1)S(1)}, bf16[2,2,48,576]{3,2,0,1:T(8,128)(2,1)S(1)}, u32[]{:S(2)}, u32[]{:S(2)}) collective-permute-start(bf16[2,2,48,576]{3,2,0,1:T(8,128)(2,1)S(1)} %bitcast.342), channel_id=1, source_target_pairs={{0,2},{1,3},{2,0},{3,1},{4,6},{5,7},{6,4},{7,5},{8,10},{9,11},{10,... | collective-permute-start | bytes 663560 | tf_op jit(solution)/shard_map/ppermute | solution.py:329
  238.0 14.3 %collective-permute-start.42 = (bf16[384,384]{1,0:T(8,128)(2,1)S(1)}, bf16[384,384]{1,0:T(8,128)(2,1)S(1)}, u32[]{:S(2)}, u32[]{:S(2)}) collective-permute-start(bf16[384,384]{1,0:T(8,128)(2,1)S(1)} %fusion.13), channel_id=1, source_target_pairs={{0,8},{1,9},{2,10},{3,11},{4,12},{5,13},{6,14},{7,15},{8,0},{9,1},... | collective-permute-start | bytes 884744 | tf_op jit(solution)/shard_map/ppermute | solution.py:329
  254.0 10.8 %collective-permute-start.44 = (bf16[192,960]{1,0:T(8,128)(2,1)S(1)}, bf16[192,960]{1,0:T(8,128)(2,1)S(1)}, u32[]{:S(2)}, u32[]{:S(2)}) collective-permute-start(bf16[192,960]{1,0:T(8,128)(2,1)S(1)} %pad_maximum_fusion.8), channel_id=1, source_target_pairs={{0,4},{1,5},{2,6},{3,7},{4,0},{5,1},{6,2},{7,3},{8,12},{9,13},{10,... | collective-permute-start | bytes 1105928 | tf_op jit(solution)/shard_map/ppermute | solution.py:329
  254.3 12.8 %collective-permute-start.43 = (bf16[288,768]{1,0:T(8,128)(2,1)S(1)}, bf16[288,768]{1,0:T(8,128)(2,1)}, u32[]{:S(2)}, u32[]{:S(2)}) collective-permute-start(bf16[288,768]{1,0:T(8,128)(2,1)S(1)} %pad_maximum_fusion.6), channel_id=1, source_target_pairs={{0,2},{1,17},{2,0},{3,19},{4,6},{5,21},{6,4},{7,23},{8,10},{9,25},... | collective-permute-start | bytes 1327112 | tf_op jit(solution)/shard_map/ppermute | solution.py:329
  255.2 13.7 %collective-permute-start.45 = (bf16[384,384]{1,0:T(8,128)(2,1)S(1)}, bf16[384,384]{1,0:T(8,128)(2,1)}, u32[]{:S(2)}, u32[]{:S(2)}) collective-permute-start(bf16[384,384]{1,0:T(8,128)(2,1)S(1)} %fusion.8), channel_id=1, source_target_pairs={{0,16},{1,17},{2,18},{3,19},{4,20},{5,21},{6,22},{7,23},{8,24},{9,... | collective-permute-start | bytes 884744 | tf_op jit(solution)/shard_map/ppermute | solution.py:329
  269.3 21.3 %collective-permute-start.48 = (bf16[192,768]{1,0:T(8,128)(2,1)S(1)}, bf16[192,768]{1,0:T(8,128)(2,1)S(1)}, u32[]{:S(2)}, u32[]{:S(2)}) collective-permute-start(bf16[192,768]{1,0:T(8,128)(2,1)S(1)} %pad_maximum_fusion.14), channel_id=1, source_target_pairs={{0,8},{1,9},{2,10},{3,11},{4,12},{5,13},{6,14},{7,15},{8,0},{9,1},... | collective-permute-start | bytes 884744 | tf_op jit(solution)/shard_map/ppermute | solution.py:329
  270.4 11.1 %collective-permute-start.46 = (bf16[160,768]{1,0:T(8,128)(2,1)S(1)}, bf16[160,768]{1,0:T(8,128)(2,1)S(1)}, u32[]{:S(2)}, u32[]{:S(2)}) collective-permute-start(bf16[160,768]{1,0:T(8,128)(2,1)S(1)} %pad_maximum_fusion.21), channel_id=1, source_target_pairs={{0,4},{1,5},{2,6},{3,7},{4,0},{5,1},{6,2},{7,3},{8,12},{9,13},{10,... | collective-permute-start | bytes 737288 | tf_op jit(solution)/shard_map/ppermute | solution.py:329
  273.2 9.0 %collective-permute-start.47 = (bf16[192,384]{1,0:T(8,128)(2,1)S(1)}, bf16[192,384]{1,0:T(8,128)(2,1)S(1)}, u32[]{:S(2)}, u32[]{:S(2)}) collective-permute-start(bf16[192,384]{1,0:T(8,128)(2,1)S(1)} %get-tuple-element.237), channel_id=1, source_target_pairs={{0,1},{1,0},{2,3},{3,2},{4,5},{5,4},{6,7},{7,6},{8,9},{9,8},{10,11... | collective-permute-start | bytes 442376 | tf_op jit(solution)/shard_map/ppermute | solution.py:329
  282.2 10.4 %collective-permute-start.49 = (f32[9,768]{1,0:T(8,128)S(1)}, f32[9,768]{1,0:T(8,128)S(1)}, u32[]{:S(2)}, u32[]{:S(2)}) collective-permute-start(f32[9,768]{1,0:T(8,128)S(1)} %convert_add_fusion.14), channel_id=1, source_target_pairs={{0,8},{1,9},{2,10},{3,11},{4,12},{5,13},{6,14},{7,15},{8,0},{9,1},... | collective-permute-start | bytes 82952 | tf_op jit(solution)/shard_map/ppermute | solution.py:329
  288.0 6.0 %collective-permute-start.50 = (bf16[64,768]{1,0:T(8,128)(2,1)}, bf16[64,768]{1,0:T(8,128)(2,1)S(1)}, u32[]{:S(2)}, u32[]{:S(2)}) collective-permute-start(bf16[64,768]{1,0:T(8,128)(2,1)} %get-tuple-element.203), channel_id=1, source_target_pairs={{0,8},{1,9},{2,10},{3,11},{4,12},{5,13},{6,14},{7,15},{8,0},{9,1},... | collective-permute-start | bytes 294920 | tf_op jit(solution)/shard_map/ppermute | solution.py:329
  295.8 8.1 %collective-permute-start.51 = (bf16[48,3072]{1,0:T(8,128)(2,1)S(1)}, bf16[48,3072]{1,0:T(8,128)(2,1)S(1)}, u32[]{:S(2)}, u32[]{:S(2)}) collective-permute-start(bf16[48,3072]{1,0:T(8,128)(2,1)S(1)} %pad_maximum_fusion.15), channel_id=1, source_target_pairs={{0,16},{1,17},{2,18},{3,19},{4,20},{5,21},{6,22},{7,23},{8,24},{9,... | collective-permute-start | bytes 884744 | tf_op jit(solution)/shard_map/ppermute | solution.py:329
  (39 other events, 241.6 us)
